TPU v7x, 128 devices: a whole 4x4x4 slice. The times are simulated.
128 devices in a mesh: sub: 32 (over y, z, core), rep: 4 (over x).
Axes of the slice: x: 4, y: 4, z: 4, core: 2. Of those that a mesh axis runs over, the one named last changes fastest.
Arguments:
- regions: bfloat16 [512, 512, 256], P('rep', 'sub'), may hold values from -6 to 6
- leaf_map: int32 [512], P('sub'), may hold values from 0 to 15, as said below
- leaf_bond_weight: bfloat16 [128, 4, 256, 1024], P(('sub', 'rep')), may hold values from -0.375 to 0.375
- mid_weight: bfloat16 [32, 4, 1024, 1024], P('sub', 'rep'), may hold values from -0.1875 to 0.1875
- upper_weight: bfloat16 [32, 1024, 2, 1024], P('sub'), may hold values from -0.1875 to 0.1875
- head_cotangent: float32 [512, 1024], P('rep', 'sub'), may hold values from -0.75 to 0.75
Outputs:
- leaf_grad: bfloat16 [128, 4, 256, 1024], P(('sub', 'rep'))
- middle_weight_gradient: bfloat16 [32, 4, 1024, 1024], P('sub', 'rep')
- upper_grad: bfloat16 [32, 1024, 2, 1024], P('sub', 'rep')
Inputs may be any that keep to these rules, and one draw needn't show every extreme that they name: `leaf_map`: each aligned block of 16 entries is a permutation of 0 .. 15.
All inputs are finite; a program needn't handle non-finite values.
Results may differ from a plain program's by a relative error of at most 0.04.
Values may be sent and summed in bfloat16 or wider, within the bound.
A program may use at most 128 MiB of HBM per device.

v0:
```python
import jax
import jax.numpy as jnp
from jax import lax
from jax.sharding import PartitionSpec as P

EPSILON = 1e-06


def partner(value, axis, bit):
    return lax.ppermute(value, axis, [(i, i ^ 1 << bit) for i in range(lax.axis_size(axis))])


def rms_factor(values):
    return lax.rsqrt(jnp.mean(values * values, axis=-1, keepdims=True) + EPSILON)


def norm_back(gradient, normed, factor):
    return factor * (gradient - normed * jnp.mean(gradient * normed, axis=-1, keepdims=True))


def product_of(factors):
    running = factors[..., 0, :]
    for position in range(1, factors.shape[-2]):
        running = running * factors[..., position, :]
    return running


def leave_one(factors):
    how_many = factors.shape[-2]
    results = []
    for position in range(how_many):
        remaining = [
            factors[..., partner_idx, :]
            for partner_idx in range(how_many)
            if partner_idx != position
        ]
        running = remaining[0]
        for factor in remaining[1:]:
            running = running * factor
        results.append(running)
    return jnp.stack(results, axis=-2)


def matmul(left_arr, right_arr):
    return jnp.dot(left_arr, right_arr, preferred_element_type=jnp.float32)


def matmul_t(left_arr, right_arr):
    return lax.dot_general(
        left_arr, right_arr, (((1,), (1,)), ((), ())), preferred_element_type=jnp.float32
    )


def inner_t(left_arr, right_arr):
    return lax.dot_general(
        left_arr, right_arr, (((0,), (0,)), ((), ())), preferred_element_type=jnp.float32
    )


def block_terms(inputs_rows, grads_all, widths):
    segments = []
    column = 0
    for level_pos in range(len(widths)):
        span = widths[level_pos]
        segments.append(
            jnp.einsum(
                "bsr,bsc->rsc",
                inputs_rows[:, level_pos],
                grads_all[:, :, column : column + span],
                preferred_element_type=jnp.float32,
            )
        )
        column = column + span
    return jnp.concatenate(segments, axis=-1)


def on_device(regions, leaf_map, leaf_bond_weight, mid_weight, upper_weight, head_cotangent):
    rows_dev = regions.shape[0]
    features = regions.shape[2]
    bond_width = upper_weight.shape[1]
    sub_count = lax.axis_size("sub")
    tree_depth = sub_count.bit_length() - 1
    sub_index = lax.axis_index("sub")
    placed = jnp.take(regions, leaf_map, axis=1).reshape(rows_dev, 4, 4, features)
    leaf_region_input = lax.all_to_all(placed, "rep", split_axis=1, concat_axis=0, tiled=True)[:, 0]
    leaf_terms = jnp.einsum(
        "zyu,yul->zyl", leaf_region_input, leaf_bond_weight[0], preferred_element_type=jnp.float32
    )
    leaf_prod = product_of(1.0 + leaf_terms)
    leaf_scale = rms_factor(leaf_prod)
    leaf_norm = leaf_prod * leaf_scale
    leaf_message_rows = leaf_norm.astype(jnp.bfloat16)
    mid_local = matmul(leaf_message_rows, mid_weight[0, 0]).astype(jnp.bfloat16)
    middle_node_terms = lax.all_to_all(
        mid_local[:, None, :], "rep", split_axis=0, concat_axis=1, tiled=True
    )
    mid_factors = 1.0 + middle_node_terms.astype(jnp.float32)
    mid_prod = product_of(mid_factors)
    mid_scale = rms_factor(mid_prod)
    mid_norm = mid_prod * mid_scale
    message = mid_norm.astype(jnp.bfloat16)
    maps = upper_weight[0]
    widths = []
    saved = []
    for tier_level in range(tree_depth):
        group_size = 2 ** (tier_level + 1)
        block_width = bond_width // group_size
        first_col = bond_width - 2 * block_width
        widths.append(block_width)
        sibling = partner(message, "sub", tier_level)
        is_right = (sub_index >> tier_level) % 2 == 1
        left_msg = jnp.where(is_right, sibling, message)
        right_msg = jnp.where(is_right, message, sibling)
        pieces = jnp.stack(
            [
                matmul(left_msg, maps[:, 0, first_col : first_col + block_width]),
                matmul(right_msg, maps[:, 1, first_col : first_col + block_width]),
            ],
            axis=0,
        )
        for bit_pos in range(tier_level + 1):
            other = partner(pieces.astype(jnp.bfloat16), "sub", bit_pos).astype(pieces.dtype)
            upper_side = (sub_index >> bit_pos) % 2 == 1
            pieces = jnp.where(
                upper_side,
                jnp.concatenate([other, pieces], axis=-1),
                jnp.concatenate([pieces, other], axis=-1),
            )
        up_left = pieces[0]
        up_right = pieces[1]
        joined = (1.0 + up_left) * (1.0 + up_right)
        scaling = rms_factor(joined)
        message = (joined * scaling).astype(jnp.bfloat16)
        saved.append((left_msg, right_msg, up_left, up_right, scaling))
    head_width = bond_width // sub_count
    head_col = bond_width - head_width
    head_left = maps[:, 0, head_col:]
    head_right = maps[:, 1, head_col:]
    head_value = matmul(message, head_left)
    gating = jax.nn.sigmoid(matmul(message, head_right))
    grad_value = (head_cotangent * gating).astype(jnp.bfloat16)
    grad_gate = (head_cotangent * head_value * gating * (1.0 - gating)).astype(jnp.bfloat16)
    root_term = matmul_t(grad_value, head_left) + matmul_t(grad_gate, head_right)
    grad_msg = lax.psum(root_term.astype(jnp.bfloat16), "sub").astype(jnp.float32)
    grad_blocks = [None] * tree_depth
    for tier_level in reversed(range(tree_depth)):
        group_size = 2 ** (tier_level + 1)
        block_width = bond_width // group_size
        first_col = bond_width - 2 * block_width
        left_msg, right_msg, up_left, up_right, scaling = saved[tier_level]
        normed = (1.0 + up_left) * (1.0 + up_right) * scaling
        joined_grad = norm_back(grad_msg, normed, scaling)
        grad_left = (joined_grad * (1.0 + up_right)).astype(jnp.bfloat16)
        grad_right = (joined_grad * (1.0 + up_left)).astype(jnp.bfloat16)
        own_start = sub_index % group_size * block_width
        left_block = lax.dynamic_slice_in_dim(grad_left, own_start, block_width, 1)
        right_block = lax.dynamic_slice_in_dim(grad_right, own_start, block_width, 1)
        grad_blocks[tier_level] = jnp.stack([left_block, right_block], axis=1)
        sums = jnp.stack(
            [
                matmul_t(left_block, maps[:, 0, first_col : first_col + block_width]),
                matmul_t(right_block, maps[:, 1, first_col : first_col + block_width]),
            ],
            axis=0,
        )
        for bit_pos in range(tier_level + 1):
            sums = sums + partner(sums.astype(jnp.bfloat16), "sub", bit_pos).astype(sums.dtype)
        is_right = (sub_index >> tier_level) % 2 == 1
        grad_msg = jnp.where(is_right, sums[1], sums[0])
    sub_back = norm_back(grad_msg, mid_norm, mid_scale)
    middle_gradient_list = (sub_back[:, None, :] * leave_one(mid_factors)).astype(jnp.bfloat16)
    child_grad = lax.all_to_all(
        middle_gradient_list, "rep", split_axis=1, concat_axis=0, tiled=True
    )[:, 0]
    middle_weight_gradient = inner_t(leaf_message_rows, child_grad).astype(jnp.bfloat16)[None, None]
    leaf_backward_pass = matmul_t(child_grad, mid_weight[0, 0])
    node_back = norm_back(leaf_backward_pass, leaf_norm, leaf_scale)
    leaf_weight_gradients = (node_back[:, None, :] * leave_one(1.0 + leaf_terms)).astype(
        jnp.bfloat16
    )
    leaf_grad = jnp.einsum(
        "yor,yon->orn", leaf_region_input, leaf_weight_gradients, preferred_element_type=jnp.float32
    ).astype(jnp.bfloat16)[None]
    widths.append(head_width)
    inputs_all = jnp.stack(
        [jnp.stack([entry[0], entry[1]], axis=1) for entry in saved]
        + [jnp.stack([message, message], axis=1)],
        axis=1,
    )
    grads_all = jnp.concatenate(grad_blocks + [jnp.stack([grad_value, grad_gate], axis=1)], axis=-1)
    upper_sum = lax.psum_scatter(
        block_terms(inputs_all, grads_all, widths).astype(jnp.bfloat16),
        "rep",
        scatter_dimension=0,
        tiled=True,
    )
    return (leaf_grad, middle_weight_gradient, upper_sum[None])


def solution(mesh):
    placed = (
        P("rep", "sub", None),
        P("sub"),
        P(("sub", "rep"), None, None, None),
        P("sub", "rep", None, None),
        P("sub", None, None, None),
        P("rep", "sub"),
    )
    return jax.shard_map(
        on_device,
        mesh=mesh,
        in_specs=placed,
        out_specs=(
            P(("sub", "rep"), None, None, None),
            P("sub", "rep", None, None),
            P("sub", "rep", None, None),
        ),
        check_vma=False,
    )
```

profile of v0, /device:TPU:1, one launch (start us, length us, event | category | flops | bytes accessed | tf_op | source)
XLA Modules:
  0.0 554.6 jit_solution(5154573626090360563)
XLA Ops:
  8.7 3.7 gather_fusion
  15.2 18.9 %all_to_all.39 = bf16[128,4,4,256]{3,0,2,1:T(8,128)(2,1)S(1)} all-to-all(bf16[128,4,4,256]{3,0,2,1:T(8,128)(2,1)S(1)} %broadcast_select_fusion), channel_id=1, replica_groups=mesh['sub'=32,'rep'=4] {'rep'}, dimensions={1} | all-to-all | bytes 2097152 | tf_op jit(solution)/shard_map/all_to_all | solution.py:85
  44.7 15.8 %all_to_all.40 = bf16[4,2,65536]{2,1,0:T(2,128)(2,1)S(1)} all-to-all(bf16[4,2,65536]{2,1,0:T(2,128)(2,1)S(1)} %reshape.272), channel_id=1, replica_groups=mesh['sub'=32,'rep'=4] {'rep'}, dimensions={0} | all-to-all | bytes 2097152 | tf_op jit(solution)/shard_map/all_to_all | solution.py:94
  66.1 2.7 collective-permute-start
  68.9 5.6 %copy.147 = bf16[1,1024,2,1024]{3,1,2,0:T(8,128)(2,1)} copy(bf16[1,1024,2,1024]{3,2,1,0:T(2,128)(2,1)} %param.10) | data formatting | bytes 8388608 | tf_op args[4]
  82.2 6.4 %collective-permute-done.2 = bf16[128,1024]{0,1:T(8,128)(2,1)S(1)} collective-permute-done((bf16[128,1024]{0,1:T(8,128)(2,1)S(1)}, bf16[128,1024]{0,1:T(8,128)(2,1)S(1)}, u32[]{:S(2)}, u32[]{:S(2)}) %collective-permute-start.2) | collective-permute-done | bytes 262176 | tf_op jit(solution)/shard_map/ppermute | solution.py:10
  95.1 6.0 %collective-permute-done.4 = bf16[2,128,512]{1,2,0:T(8,128)(2,1)S(1)} collective-permute-done((bf16[2,128,512]{1,2,0:T(8,128)(2,1)S(1)}, bf16[2,128,512]{1,2,0:T(8,128)(2,1)S(1)}, u32[]{:S(2)}, u32[]{:S(2)}) %collective-permute-start.4) | collective-permute-done | bytes 262176 | tf_op jit(solution)/shard_map/ppermute | solution.py:10
  101.6 3.5 collective-permute-start.5
  105.1 5.5 collective-permute-done.5
  117.0 3.7 collective-permute-done.7
  120.9 3.0 collective-permute-start.8
  123.9 5.2 collective-permute-done.8
  131.8 4.5 collective-permute-done.9
  138.8 3.0 collective-permute-start.10
  146.0 3.0 collective-permute-start.12
  152.9 3.9 collective-permute-done.13
  157.2 3.0 collective-permute-start.14
  160.2 5.0 collective-permute-done.14
  167.8 3.9 collective-permute-start.15
  175.4 3.0 collective-permute-start.17
  181.6 2.5 collective-permute-done.18
  184.2 3.7 collective-permute-start.19
  187.9 5.2 collective-permute-done.19
  200.1 107.1 %all-reduce.2.cloned.1.call-done = bf16[128,1024]{0,1:T(8,128)(2,1)} async-done(((bf16[128,1024]{0,1:T(8,128)(2,1)}), bf16[128,1024]{0,1:T(8,128)(2,1)}) %all-reduce.2.cloned.1.call-update) | async-done | bytes 262160 | tf_op jit(solution)/shard_map/psum | solution.py:144
  315.8 12.6 %collective-permute-done.21 = bf16[2,128,1024]{1,2,0:T(8,128)(2,1)S(1)} collective-permute-done((bf16[2,128,1024]{1,2,0:T(8,128)(2,1)S(1)}, bf16[2,128,1024]{1,2,0:T(8,128)(2,1)S(1)}, u32[]{:S(2)}, u32[]{:S(2)}) %collective-permute-start.21) | collective-permute-done | bytes 524320 | tf_op jit(solution)/shard_map/ppermute | solution.py:10
  328.6 2.5 collective-permute-start.22
  331.2 11.3 %collective-permute-done.22 = bf16[2,128,1024]{1,2,0:T(8,128)(2,1)S(1)} collective-permute-done((bf16[2,128,1024]{1,2,0:T(8,128)(2,1)S(1)}, bf16[2,128,1024]{1,2,0:T(8,128)(2,1)S(1)}, u32[]{:S(2)}, u32[]{:S(2)}) %collective-permute-start.22) | collective-permute-done | bytes 524320 | tf_op jit(solution)/shard_map/ppermute | solution.py:10
  343.4 10.8 %collective-permute-done.23 = bf16[2,128,1024]{1,2,0:T(8,128)(2,1)S(1)} collective-permute-done((bf16[2,128,1024]{1,2,0:T(8,128)(2,1)S(1)}, bf16[2,128,1024]{1,2,0:T(8,128)(2,1)S(1)}, u32[]{:S(2)}, u32[]{:S(2)}) %collective-permute-start.23) | collective-permute-done | bytes 524320 | tf_op jit(solution)/shard_map/ppermute | solution.py:10
  355.1 3.2 collective-permute-start.24
  359.6 8.2 %collective-permute-done.24 = bf16[2,128,1024]{1,2,0:T(8,128)(2,1)} collective-permute-done((bf16[2,128,1024]{1,2,0:T(8,128)(2,1)}, bf16[2,128,1024]{1,2,0:T(8,128)(2,1)}, u32[]{:S(2)}, u32[]{:S(2)}) %collective-permute-start.24) | collective-permute-done | bytes 524320 | tf_op jit(solution)/shard_map/ppermute | solution.py:10
  371.7 3.7 collective-permute-start.25
  378.0 12.3 %collective-permute-done.26 = bf16[2,128,1024]{1,2,0:T(8,128)(2,1)S(1)} collective-permute-done((bf16[2,128,1024]{1,2,0:T(8,128)(2,1)S(1)}, bf16[2,128,1024]{1,2,0:T(8,128)(2,1)S(1)}, u32[]{:S(2)}, u32[]{:S(2)}) %collective-permute-start.26) | collective-permute-done | bytes 524320 | tf_op jit(solution)/shard_map/ppermute | solution.py:10
  390.5 2.8 collective-permute-start.27
  393.2 11.1 %collective-permute-done.27 = bf16[2,128,1024]{1,2,0:T(8,128)(2,1)S(1)} collective-permute-done((bf16[2,128,1024]{1,2,0:T(8,128)(2,1)S(1)}, bf16[2,128,1024]{1,2,0:T(8,128)(2,1)S(1)}, u32[]{:S(2)}, u32[]{:S(2)}) %collective-permute-start.27) | collective-permute-done | bytes 524320 | tf_op jit(solution)/shard_map/ppermute | solution.py:10
  407.4 9.7 %collective-permute-done.28 = bf16[2,128,1024]{1,2,0:T(8,128)(2,1)} collective-permute-done((bf16[2,128,1024]{1,2,0:T(8,128)(2,1)}, bf16[2,128,1024]{1,2,0:T(8,128)(2,1)}, u32[]{:S(2)}, u32[]{:S(2)}) %collective-permute-start.28) | collective-permute-done | bytes 524320 | tf_op jit(solution)/shard_map/ppermute | solution.py:10
  421.2 3.0 collective-permute-start.29
  426.8 12.3 %collective-permute-done.30 = bf16[2,128,1024]{1,2,0:T(8,128)(2,1)S(1)} collective-permute-done((bf16[2,128,1024]{1,2,0:T(8,128)(2,1)S(1)}, bf16[2,128,1024]{1,2,0:T(8,128)(2,1)S(1)}, u32[]{:S(2)}, u32[]{:S(2)}) %collective-permute-start.30) | collective-permute-done | bytes 524320 | tf_op jit(solution)/shard_map/ppermute | solution.py:10
  440.9 2.7 collective-permute-start.31
  446.1 8.9 %collective-permute-done.31 = bf16[2,128,1024]{1,2,0:T(8,128)(2,1)} collective-permute-done((bf16[2,128,1024]{1,2,0:T(8,128)(2,1)}, bf16[2,128,1024]{1,2,0:T(8,128)(2,1)}, u32[]{:S(2)}, u32[]{:S(2)}) %collective-permute-start.31) | collective-permute-done | bytes 524320 | tf_op jit(solution)/shard_map/ppermute | solution.py:10
  464.5 12.0 %collective-permute-done.33 = bf16[2,128,1024]{1,2,0:T(8,128)(2,1)S(1)} collective-permute-done((bf16[2,128,1024]{1,2,0:T(8,128)(2,1)S(1)}, bf16[2,128,1024]{1,2,0:T(8,128)(2,1)S(1)}, u32[]{:S(2)}, u32[]{:S(2)}) %collective-permute-start.33) | collective-permute-done | bytes 524320 | tf_op jit(solution)/shard_map/ppermute | solution.py:10
  493.6 4.0 all-to-all-start.2
  497.6 7.9 %multiply_multiply_fusion.1 = (f32[512,1,1024]{2,0,1:T(8,128)}, f32[512,1,1024]{2,0,1:T(8,128)}, f32[512,1,1024]{2,0,1:T(8,128)}) fusion(f32[512,4,1024]{2,0,1:T(8,128)} %copy-done.2), kind=kLoop, calls=%fused_computation.20 | loop fusion | flops 3145728 | bytes 14680064 | tf_op jit(solution)/shard_map/mul | solution.py:39
  505.5 18.8 %all-to-all-done.2 = bf16[128,4,1024]{2,0,1:T(8,128)(2,1)S(1)} async-done(((bf16[128,4,1024]{2,0,1:T(8,128)(2,1)}), bf16[128,4,1024]{2,0,1:T(8,128)(2,1)S(1)}, u32[]{:S(2)}, u32[]{:S(2)}) %all-to-all-start.2) | async-done | bytes 1048608 | tf_op jit(solution)/shard_map/all_to_all | solution.py:172
  524.3 3.0 multiply_reduce_fusion
  527.3 2.7 convert_bitcast_fusion
  532.5 2.5 convert_bitcast_fusion.1
  535.1 8.8 %reduce-scatter.2.cloned.1.call-done = bf16[256,2,1024]{0,2,1:T(8,128)(2,1)} async-done(((bf16[1024,2,1024]{0,2,1:T(8,128)(2,1)}), bf16[256,2,1024]{0,2,1:T(8,128)(2,1)}) %reduce-scatter.2.cloned.1.call-update) | async-done | bytes 1048592 | tf_op jit(solution)/shard_map/reduce_scatter | solution.py:191
  543.9 3.7 copy.117
  (304 shorter events, 132.9 us)
Async XLA Ops:
  7.2 28.0 %copy-start = (bf16[1,4,256,1024]{3,2,1,0:T(8,128)(2,1)S(1)}, bf16[1,4,256,1024]{3,2,1,0:T(8,128)(2,1)}, u32[]{:S(2)}) copy-start(bf16[1,4,256,1024]{3,2,1,0:T(8,128)(2,1)} %param.8) | copy-start | bytes 6291460
  7.2 300.1 %all-reduce.2.cloned.1.call-start = ((), (), s32[]{:S(2)}) async-start(), calls=%async_computation.4 | async-start | bytes 524288 | tf_op jit(solution)/shard_map/psum | solution.py:144
  66.1 8.3 %collective-permute-start = (bf16[128,1024]{1,0:T(8,128)(2,1)S(1)}, bf16[128,1024]{1,0:T(8,128)(2,1)S(1)}, u32[]{:S(2)}, u32[]{:S(2)}) collective-permute-start(bf16[128,1024]{1,0:T(8,128)(2,1)S(1)} %fusion.83), channel_id=1, source_target_pairs={{0,4},{4,0},{8,12},{12,8},{16,20},{20,16},{24,28},{28,24},{32,36},... | collective-permute-start | bytes 786440 | tf_op jit(solution)/shard_map/ppermute | solution.py:10
  78.0 2.1 collective-permute-start.1
  80.5 8.2 %collective-permute-start.2 = (bf16[128,1024]{0,1:T(8,128)(2,1)S(1)}, bf16[128,1024]{0,1:T(8,128)(2,1)S(1)}, u32[]{:S(2)}, u32[]{:S(2)}) collective-permute-start(bf16[128,1024]{0,1:T(8,128)(2,1)S(1)} %multiply_convert_fusion.5), channel_id=1, source_target_pairs={{0,8},{4,12},{8,0},{12,4},{16,24},{20,28},{24,16},{28,20},{32,40},... | collective-permute-start | bytes 786440 | tf_op jit(solution)/shard_map/ppermute | solution.py:10
  91.5 1.9 collective-permute-start.3
  93.6 7.6 %collective-permute-start.4 = (bf16[2,128,512]{1,2,0:T(8,128)(2,1)S(1)}, bf16[2,128,512]{1,2,0:T(8,128)(2,1)S(1)}, u32[]{:S(2)}, u32[]{:S(2)}) collective-permute-start(bf16[2,128,512]{1,2,0:T(8,128)(2,1)S(1)} %get-tuple-element.41), channel_id=1, source_target_pairs={{0,8},{4,12},{8,0},{12,4},{16,24},{20,28},{24,16},{28,20},{32,40},... | collective-permute-start | bytes 786440 | tf_op jit(solution)/shard_map/ppermute | solution.py:10
  101.6 9.0 %collective-permute-start.5 = (bf16[128,1024]{0,1:T(8,128)(2,1)S(1)}, bf16[128,1024]{0,1:T(8,128)(2,1)S(1)}, u32[]{:S(2)}, u32[]{:S(2)}) collective-permute-start(bf16[128,1024]{0,1:T(8,128)(2,1)S(1)} %multiply_convert_fusion.4), channel_id=1, source_target_pairs={{0,16},{4,20},{8,24},{12,28},{16,0},{20,4},{24,8},{28,12},{32,48},... | collective-permute-start | bytes 786440 | tf_op jit(solution)/shard_map/ppermute | solution.py:10
  113.1 2.8 collective-permute-start.6
  115.9 4.8 collective-permute-start.7
  120.9 8.2 %collective-permute-start.8 = (bf16[2,128,512]{1,2,0:T(8,128)(2,1)S(1)}, bf16[2,128,512]{1,2,0:T(8,128)(2,1)S(1)}, u32[]{:S(2)}, u32[]{:S(2)}) collective-permute-start(bf16[2,128,512]{1,2,0:T(8,128)(2,1)S(1)} %get-tuple-element.35), channel_id=1, source_target_pairs={{0,16},{4,20},{8,24},{12,28},{16,0},{20,4},{24,8},{28,12},{32,48},... | collective-permute-start | bytes 786440 | tf_op jit(solution)/shard_map/ppermute | solution.py:10
  130.4 21.0 %copy-start.7 = (f32[128,1024]{0,1:T(8,128)}, f32[128,1024]{0,1:T(8,128)S(1)}, u32[]{:S(2)}) copy-start(f32[128,1024]{0,1:T(8,128)S(1)} %get-tuple-element.34) | copy-start | bytes 1572868
  130.4 288.3 %copy-start.48 = (f32[128]{0:T(128)}, f32[128]{0:T(128)S(1)}, u32[]{:S(2)}) copy-start(f32[128]{0:T(128)S(1)} %add_rsqrt_fusion.3) | copy-start | bytes 1540
  130.5 5.9 %collective-permute-start.9 = (bf16[128,1024]{0,1:T(8,128)(2,1)S(1)}, bf16[128,1024]{0,1:T(8,128)(2,1)S(1)}, u32[]{:S(2)}, u32[]{:S(2)}) collective-permute-start(bf16[128,1024]{0,1:T(8,128)(2,1)S(1)} %multiply_convert_fusion.3), channel_id=1, source_target_pairs={{0,32},{4,36},{8,40},{12,44},{16,48},{20,52},{24,56},{28,60},{32,0... | collective-permute-start | bytes 786440 | tf_op jit(solution)/shard_map/ppermute | solution.py:10
  138.8 3.9 collective-permute-start.10
  142.7 3.2 collective-permute-start.11
  146.0 5.4 collective-permute-start.12
  151.5 5.3 collective-permute-start.13
  157.0 15.6 %copy-start.18 = (f32[2,128,1024]{1,2,0:T(8,128)}, f32[2,128,1024]{1,2,0:T(8,128)S(1)}, u32[]{:S(2)}) copy-start(f32[2,128,1024]{1,2,0:T(8,128)S(1)} %maximum_select_fusion.3) | copy-start | bytes 3145732
  157.2 212.1 %copy-start.10 = (f32[128,1024]{0,1:T(8,128)}, f32[128,1024]{0,1:T(8,128)S(1)}, u32[]{:S(2)}) copy-start(f32[128,1024]{0,1:T(8,128)S(1)} %get-tuple-element.26) | copy-start | bytes 1572868
  157.2 212.1 %copy-start.50 = (f32[128]{0:T(128)}, f32[128]{0:T(128)S(1)}, u32[]{:S(2)}) copy-start(f32[128]{0:T(128)S(1)} %add_rsqrt_fusion.2) | copy-start | bytes 1540
  157.2 8.0 %collective-permute-start.14 = (bf16[128,1024]{0,1:T(8,128)(2,1)S(1)}, bf16[128,1024]{0,1:T(8,128)(2,1)S(1)}, u32[]{:S(2)}, u32[]{:S(2)}) collective-permute-start(bf16[128,1024]{0,1:T(8,128)(2,1)S(1)} %multiply_convert_fusion.2), channel_id=1, source_target_pairs={{0,64},{4,68},{8,72},{12,76},{16,80},{20,84},{24,88},{28,92},{32,9... | collective-permute-start | bytes 786440 | tf_op jit(solution)/shard_map/ppermute | solution.py:10
  165.2 19.0 %copy-start.45 = (bf16[128,1024]{0,1:T(8,128)(2,1)}, bf16[128,1024]{0,1:T(8,128)(2,1)S(1)}, u32[]{:S(2)}) copy-start(bf16[128,1024]{0,1:T(8,128)(2,1)S(1)} %collective-permute-done.14) | copy-start | bytes 786436
  167.8 4.7 collective-permute-start.15
  172.6 2.8 collective-permute-start.16
  175.4 4.7 collective-permute-start.17
  180.2 3.9 collective-permute-start.18
  184.2 8.9 %collective-permute-start.19 = (bf16[2,128,512]{1,2,0:T(8,128)(2,1)S(1)}, bf16[2,128,512]{1,2,0:T(8,128)(2,1)S(1)}, u32[]{:S(2)}, u32[]{:S(2)}) collective-permute-start(bf16[2,128,512]{1,2,0:T(8,128)(2,1)S(1)} %get-tuple-element.17), channel_id=1, source_target_pairs={{0,64},{4,68},{8,72},{12,76},{16,80},{20,84},{24,88},{28,92},{32,9... | collective-permute-start | bytes 786440 | tf_op jit(solution)/shard_map/ppermute | solution.py:10
  193.4 114.9 %copy-start.52 = (f32[128]{0:T(128)}, f32[128]{0:T(128)S(1)}, u32[]{:S(2)}) copy-start(f32[128]{0:T(128)S(1)} %add_rsqrt_fusion.1) | copy-start | bytes 1540
  200.1 343.8 %reduce-scatter.2.cloned.1.call-start = ((), (), s32[]{:S(2)}) async-start(), calls=%async_computation.5 | async-start | bytes 5242880 | tf_op jit(solution)/shard_map/reduce_scatter | solution.py:191
  312.7 2.2 collective-permute-start.20
  315.1 13.4 %collective-permute-start.21 = (bf16[2,128,1024]{1,2,0:T(8,128)(2,1)S(1)}, bf16[2,128,1024]{1,2,0:T(8,128)(2,1)S(1)}, u32[]{:S(2)}, u32[]{:S(2)}) collective-permute-start(bf16[2,128,1024]{1,2,0:T(8,128)(2,1)S(1)} %fusion.120), channel_id=1, source_target_pairs={{0,8},{4,12},{8,0},{12,4},{16,24},{20,28},{24,16},{28,20},{32,40},... | collective-permute-start | bytes 1572872 | tf_op jit(solution)/shard_map/ppermute | solution.py:10
  328.6 13.8 %collective-permute-start.22 = (bf16[2,128,1024]{1,2,0:T(8,128)(2,1)S(1)}, bf16[2,128,1024]{1,2,0:T(8,128)(2,1)S(1)}, u32[]{:S(2)}, u32[]{:S(2)}) collective-permute-start(bf16[2,128,1024]{1,2,0:T(8,128)(2,1)S(1)} %fusion.41), channel_id=1, source_target_pairs={{0,16},{4,20},{8,24},{12,28},{16,0},{20,4},{24,8},{28,12},{32,48},... | collective-permute-start | bytes 1572872 | tf_op jit(solution)/shard_map/ppermute | solution.py:10
  342.7 11.5 %collective-permute-start.23 = (bf16[2,128,1024]{1,2,0:T(8,128)(2,1)S(1)}, bf16[2,128,1024]{1,2,0:T(8,128)(2,1)S(1)}, u32[]{:S(2)}, u32[]{:S(2)}) collective-permute-start(bf16[2,128,1024]{1,2,0:T(8,128)(2,1)S(1)} %get-tuple-element.15), channel_id=1, source_target_pairs={{0,32},{4,36},{8,40},{12,44},{16,48},{20,52},{24,56},{28,60},{32,0... | collective-permute-start | bytes 1572872 | tf_op jit(solution)/shard_map/ppermute | solution.py:10
  355.1 12.8 %collective-permute-start.24 = (bf16[2,128,1024]{1,2,0:T(8,128)(2,1)}, bf16[2,128,1024]{1,2,0:T(8,128)(2,1)}, u32[]{:S(2)}, u32[]{:S(2)}) collective-permute-start(bf16[2,128,1024]{1,2,0:T(8,128)(2,1)} %fusion.42), channel_id=1, source_target_pairs={{0,64},{4,68},{8,72},{12,76},{16,80},{20,84},{24,88},{28,92},{32,9... | collective-permute-start | bytes 1572872 | tf_op jit(solution)/shard_map/ppermute | solution.py:10
  371.7 5.2 collective-permute-start.25
  377.0 27.4 %copy-start.21 = (bf16[2,128,1024]{1,2,0:T(8,128)(2,1)}, bf16[2,128,1024]{1,2,0:T(8,128)(2,1)S(1)}, u32[]{:S(2)}) copy-start(bf16[2,128,1024]{1,2,0:T(8,128)(2,1)S(1)} %collective-permute-done.25) | copy-start | bytes 1572868
  377.1 13.2 %collective-permute-start.26 = (bf16[2,128,1024]{1,2,0:T(8,128)(2,1)S(1)}, bf16[2,128,1024]{1,2,0:T(8,128)(2,1)S(1)}, u32[]{:S(2)}, u32[]{:S(2)}) collective-permute-start(bf16[2,128,1024]{1,2,0:T(8,128)(2,1)S(1)} %fusion.144), channel_id=1, source_target_pairs={{0,8},{4,12},{8,0},{12,4},{16,24},{20,28},{24,16},{28,20},{32,40},... | collective-permute-start | bytes 1572872 | tf_op jit(solution)/shard_map/ppermute | solution.py:10
  390.5 13.8 %collective-permute-start.27 = (bf16[2,128,1024]{1,2,0:T(8,128)(2,1)S(1)}, bf16[2,128,1024]{1,2,0:T(8,128)(2,1)S(1)}, u32[]{:S(2)}, u32[]{:S(2)}) collective-permute-start(bf16[2,128,1024]{1,2,0:T(8,128)(2,1)S(1)} %fusion.43), channel_id=1, source_target_pairs={{0,16},{4,20},{8,24},{12,28},{16,0},{20,4},{24,8},{28,12},{32,48},... | collective-permute-start | bytes 1572872 | tf_op jit(solution)/shard_map/ppermute | solution.py:10
  405.4 11.7 %collective-permute-start.28 = (bf16[2,128,1024]{1,2,0:T(8,128)(2,1)}, bf16[2,128,1024]{1,2,0:T(8,128)(2,1)}, u32[]{:S(2)}, u32[]{:S(2)}) collective-permute-start(bf16[2,128,1024]{1,2,0:T(8,128)(2,1)} %fusion.87), channel_id=1, source_target_pairs={{0,32},{4,36},{8,40},{12,44},{16,48},{20,52},{24,56},{28,60},{32,0... | collective-permute-start | bytes 1572872 | tf_op jit(solution)/shard_map/ppermute | solution.py:10
  421.2 4.6 collective-permute-start.29
  425.9 13.2 %collective-permute-start.30 = (bf16[2,128,1024]{1,2,0:T(8,128)(2,1)S(1)}, bf16[2,128,1024]{1,2,0:T(8,128)(2,1)S(1)}, u32[]{:S(2)}, u32[]{:S(2)}) collective-permute-start(bf16[2,128,1024]{1,2,0:T(8,128)(2,1)S(1)} %fusion.121), channel_id=1, source_target_pairs={{0,8},{4,12},{8,0},{12,4},{16,24},{20,28},{24,16},{28,20},{32,40},... | collective-permute-start | bytes 1572872 | tf_op jit(solution)/shard_map/ppermute | solution.py:10
  440.9 14.1 %collective-permute-start.31 = (bf16[2,128,1024]{1,2,0:T(8,128)(2,1)}, bf16[2,128,1024]{1,2,0:T(8,128)(2,1)}, u32[]{:S(2)}, u32[]{:S(2)}) collective-permute-start(bf16[2,128,1024]{1,2,0:T(8,128)(2,1)} %fusion.44), channel_id=1, source_target_pairs={{0,16},{4,20},{8,24},{12,28},{16,0},{20,4},{24,8},{28,12},{32,48},... | collective-permute-start | bytes 1572872 | tf_op jit(solution)/shard_map/ppermute | solution.py:10
  459.5 3.7 collective-permute-start.32
  463.3 13.2 %collective-permute-start.33 = (bf16[2,128,1024]{1,2,0:T(8,128)(2,1)S(1)}, bf16[2,128,1024]{1,2,0:T(8,128)(2,1)S(1)}, u32[]{:S(2)}, u32[]{:S(2)}) collective-permute-start(bf16[2,128,1024]{1,2,0:T(8,128)(2,1)S(1)} %fusion.45), channel_id=1, source_target_pairs={{0,8},{4,12},{8,0},{12,4},{16,24},{20,28},{24,16},{28,20},{32,40},... | collective-permute-start | bytes 1572872 | tf_op jit(solution)/shard_map/ppermute | solution.py:10
  488.1 3.1 collective-permute-start.34
  493.6 30.6 %all-to-all-start.2 = ((bf16[128,4,1024]{2,0,1:T(8,128)(2,1)}), bf16[128,4,1024]{2,0,1:T(8,128)(2,1)S(1)}, u32[]{:S(2)}, u32[]{:S(2)}) async-start(bf16[128,4,1024]{2,0,1:T(8,128)(2,1)} %fusion.3), calls=%async_computation.2 | async-start | bytes 2097152 | tf_op jit(solution)/shard_map/all_to_all | solution.py:172
  497.6 26.7 %copy-start.6 = (f32[512,1,1024]{2,0,1:T(8,128)S(1)}, f32[512,1,1024]{2,0,1:T(8,128)}, u32[]{:S(2)}) copy-start(f32[512,1,1024]{2,0,1:T(8,128)} %copy-done.5) | copy-start | bytes 6291460
  (44 other events, 254.0 us)
Sparse Core Ops, SparseCore 0:
  200.2 106.9 all-reduce.1
  484.6 59.2 reduce-scatter.1
where the time goes:
time: 565 us; the launch traced here: 555 us
  waiting for transfers between devices  312 us (55%)
  starting transfers between devices  73.9 us (13%)
  matrix products  51.2 us (9%)
  other arithmetic  41.3 us (7%)
  blocking collectives  34.7 us (6%)
  local copies, waits for them, and re-layouts  26.1 us (5%)
  between operations  15.4 us (3%)
    ppermute x35, waiting for transfers between devices, partner(): lax.ppermute(value, axis, [(i, i ^ 1 << bit) for i in range(lax.axis_size...  177 us
    psum x1, waiting for transfers between devices, on_device(): lax.psum(root_term.astype(jnp.bfloat16), 'sub').astype(jnp.float32)  107 us
    ppermute x35, starting transfers between devices, partner(): lax.ppermute(value, axis, [(i, i ^ 1 << bit) for i in range(lax.axis_size...  69.9 us
    unnamed x113, local copies, waits for them, and re-layouts  20.4 us
    dot_general x13, matrix products, matmul_t(): lax.dot_general(left_arr, right_arr, (((1,), (1,)), ((), ())), preferred_...  19.4 us
    all_to_all x1, blocking collectives, on_device(): lax.all_to_all(placed, 'rep', split_axis=1, concat_axis=0, tiled=True)[:, 0]  18.9 us
    all_to_all x1, waiting for transfers between devices, on_device(): lax.all_to_all(middle_gradient_list, 'rep', split_axis=1, concat_axis=0,...  18.8 us
    dot_general x13, matrix products, matmul(): return jnp.dot(left_arr, right_arr, preferred_element_type=jnp.float32)  17.8 us
  transfers between devices with their start and end apart: 38, of which 37 were waited for; matrix products, arithmetic and copies ran while one was open for 6% of the time, Pallas kernels for 0%

commit v1 on v0

v1 whole, which is shorter than its diff:
```python
import jax
import jax.numpy as jnp
from jax import lax
from jax.experimental import pallas as pl
from jax.experimental.pallas import tpu as pltpu
from jax.sharding import PartitionSpec as P

F32 = jnp.float32
BF = jnp.bfloat16
MESH = pl.DeviceIdType.MESH
EPSILON = 1e-06
D = 1024
F = 256
B = 128
REPS = 4
SUBS = 32
LEVELS = 5
ALL = REPS * B
WIDTH = [D // 2 ** (j + 1) for j in range(LEVELS)] + [D // SUBS]
COLUMN = [D - 2 * WIDTH[j] for j in range(LEVELS)] + [D - D // SUBS]
CHUNK = [2 * WIDTH[j] for j in range(LEVELS)] + [WIDTH[5]]
GROUP = [2 ** (j + 1) for j in range(LEVELS)] + [SUBS]


def nn(a, b):
    return jnp.dot(a, b, preferred_element_type=F32)


def nt(a, b):
    return lax.dot_general(a, b, (((1,), (1,)), ((), ())), preferred_element_type=F32)


def fold(values):
    return jnp.sum(values.reshape(values.shape[0] // 8, 8, values.shape[1]), axis=0)


def column_sum(values):
    return jnp.sum(values, axis=0, keepdims=True)


def factor_of(squares):
    return lax.rsqrt(column_sum(squares) * (1.0 / D) + EPSILON)


def at(index, size):
    return pl.ds(pl.multiple_of(index * size, size), size)


def others(f):
    p01 = f[0] * f[1]
    p23 = f[2] * f[3]
    return [f[1] * p23, f[0] * p23, p01 * f[3], p01 * f[2]]


def split_tile(row):
    high = row.astype(BF).astype(F32)
    index = lax.broadcasted_iota(jnp.int32, (16, B), 0)
    tile = jnp.where(index == 0, high, jnp.where(index == 1, row - high, 0.0))
    return tile.astype(BF)


def kernel(
    map_ref, reg_hbm, lw_hbm, mw_hbm, uw_hbm, cot_hbm,
    lg_hbm, mg_hbm, ug_hbm,
    R, Q, XS, XR, LW, LWT, MW, MWT, UW, WN, WT, COT, FK, LP, RL, LM, MS, MR, MP,
    A0, A1, A2, A3, A4, A5, UL, UR, JJ, GP, GB,
    BS0, BS1, BS2, BS3, BS4, BS5, BR0, BR1, BR2, BR3, BR4, BR5,
    GX, AX, CS, CR, LB, CT, XT, OU, OI,
    load_sem, local_sem, x1s, x1r, x2s, x2r, x3s, x3r, fs, fr, bs, br, axs, axr, gxs, gxr, out_sem,
):
    A = [A0, A1, A2, A3, A4, A5]
    BS = [BS0, BS1, BS2, BS3, BS4, BS5]
    BR = [BR0, BR1, BR2, BR3, BR4, BR5]
    s = lax.axis_index("sub")
    p = lax.axis_index("rep")

    def to_rep(src, dst, send, recv, peer):
        pltpu.make_async_remote_copy(
            src_ref=src, dst_ref=dst, send_sem=send, recv_sem=recv,
            device_id={"rep": peer}, device_id_type=MESH,
        ).start()

    def to_sub(src, dst, send, recv, peer):
        pltpu.make_async_remote_copy(
            src_ref=src, dst_ref=dst, send_sem=send, recv_sem=recv,
            device_id={"sub": peer}, device_id_type=MESH,
        ).start()

    def await_bytes(ref, sem):
        pltpu.make_async_copy(ref, ref, sem).wait()

    loads = [
        pltpu.make_async_copy(src, dst, load_sem.at[i])
        for i, (src, dst) in enumerate(
            [(reg_hbm, R), (lw_hbm, LW), (mw_hbm, MW), (uw_hbm, UW), (cot_hbm, COT)]
        )
    ]
    for load in loads:
        load.start()

    barrier = pltpu.get_barrier_semaphore()

    def greet_sub(i, carry):
        pl.semaphore_signal(
            barrier, inc=1, device_id={"sub": lax.rem(s + i, SUBS)}, device_id_type=MESH
        )
        return carry

    def greet_rep(i, carry):
        pl.semaphore_signal(
            barrier, inc=1, device_id={"rep": lax.rem(p + i, REPS)}, device_id_type=MESH
        )
        return carry

    lax.fori_loop(1, SUBS, greet_sub, 0)
    lax.fori_loop(1, REPS, greet_rep, 0)

    column = lax.broadcasted_iota(jnp.int32, (16, 256), 1)
    sample = lax.broadcasted_iota(jnp.int32, (16, 256), 0)
    for l in range(16):
        wanted = sample * 16 + map_ref[l]
        Q[16 * l : 16 * l + 16, :] = jnp.where(column == wanted, 1.0, 0.0).astype(BF)
    loads[0].wait()

    def place(q, carry):
        got = nn(Q[...], R[at(q, 256), :]).astype(BF)
        for l in range(16):
            XS[l // 4, l % 4, at(q, 16), :] = got[16 * l : 16 * l + 16, :]
        return carry

    lax.fori_loop(0, 8, place, 0)
    pl.semaphore_wait(barrier, SUBS - 1 + REPS - 1)

    def send_slots(i, carry):
        peer = lax.rem(p + i, REPS)
        to_rep(XS.at[peer], XR.at[:, at(p, B), :], x1s, x1r.at[p], peer)
        return carry

    lax.fori_loop(1, REPS, send_slots, 0)
    own_slots = pltpu.make_async_copy(XS.at[p], XR.at[:, at(p, B), :], local_sem.at[0])
    own_slots.start()

    GP[...] = jnp.zeros(GP.shape, BF)
    loads[1].wait()

    def turn_leaf(i, carry):
        k, t = i // 4, lax.rem(i, 4)
        LWT[k, at(t, 256), :] = LW[k, :, at(t, 256)].T
        return carry

    lax.fori_loop(0, 16, turn_leaf, 0)
    loads[2].wait()

    def turn_mid(i, carry):
        a, b = i // 4, lax.rem(i, 4)
        MWT[at(b, 256), at(a, 256)] = MW[at(a, 256), at(b, 256)].T
        return carry

    lax.fori_loop(0, 16, turn_mid, 0)

    def source(i):
        return lax.rem(p + i + i // 2 - 2 * (i // 3), REPS)

    def leaf_chunk(i):
        src = source(i)
        lanes = at(src, B)

        def terms(t, squares):
            rows = at(t, 256)
            product = None
            for k in range(4):
                factor = 1.0 + nt(LWT[k, rows, :], XR[k, lanes, :])
                FK[k, rows, lanes] = factor
                product = factor if product is None else product * factor
            LP[rows, lanes] = product
            return squares + fold(product * product)

        r = factor_of(lax.fori_loop(0, 4, terms, jnp.zeros((8, B), F32)))
        RL[:, lanes] = jnp.broadcast_to(r, (8, B))

        def scale(t, carry):
            rows = at(t, 256)
            h = LP[rows, lanes] * r
            LP[rows, lanes] = h
            LM[rows, lanes] = h.astype(BF)
            return carry

        lax.fori_loop(0, 4, scale, 0)

        def mid(t, carry):
            rows = at(t, 256)
            MS[src, rows, :] = nn(MWT[rows, :], LM[:, lanes]).astype(BF)
            return carry

        lax.fori_loop(0, 4, mid, 0)

    def turn_slots(i):
        lanes = at(source(i), B)
        for k in range(4):
            XT[k, :, lanes] = XR[k, lanes, :].T

    own_slots.wait()
    leaf_chunk(0)
    own_mid = pltpu.make_async_copy(MS.at[p], MR.at[p], local_sem.at[1])
    own_mid.start()
    loads[3].wait()

    def turn_upper(t, carry):
        rows = at(t, 128)
        for side in range(2):
            block = UW[rows, side, :]
            WN[side, rows, :] = block
            WT[side, :, rows] = block.T
        return carry

    lax.fori_loop(0, 8, turn_upper, 0)
    turn_slots(0)

    def other_chunk(i, carry):
        src = source(i)
        await_bytes(XR.at[:, at(src, B), :], x1r.at[src])
        leaf_chunk(i)
        to_rep(MS.at[src], MR.at[p], x2s, x2r, src)
        turn_slots(i)
        return carry

    lax.fori_loop(1, REPS, other_chunk, 0)

    own_mid.wait()
    await_bytes(MR.at[0:3], x2r)
    base = lax.rem(s, 2) * D

    def mid_product(t, carry):
        rows = at(t, 128)
        product = 1.0 + MR[0, rows, :].astype(F32)
        for k in range(1, 4):
            product = product * (1.0 + MR[k, rows, :].astype(F32))
        MP[rows, :] = product
        A0[pl.ds(pl.multiple_of(base + t * 128, 128), 128), :] = product.astype(BF)
        return carry

    lax.fori_loop(0, 8, mid_product, 0)

    def spread(level, me, block):
        group = GROUP[level]

        def one(i, carry):
            peer = s - me + lax.rem(me + i, group)
            ref = A[level].at[at(me, block), :]
            to_sub(ref, ref, fs.at[level], fr.at[level], peer)
            return carry

        lax.fori_loop(1, group, one, 0)

    def share_rows(level):
        sides = 2 if level < LEVELS else 1

        def one(i, carry):
            peer = lax.rem(p + i, REPS)
            for side in range(sides):
                rows = pl.ds(pl.multiple_of(side * D + peer * 256, 256), 256)
                to_rep(
                    A[level].at[rows, :], AX.at[level, side, :, at(p, B)],
                    axs.at[level], axr.at[level], peer,
                )
            return carry

        lax.fori_loop(1, REPS, one, 0)
        for side in range(sides):
            rows = pl.ds(pl.multiple_of(side * D + p * 256, 256), 256)
            copy = pltpu.make_async_copy(
                A[level].at[rows, :], AX.at[level, side, :, at(p, B)], local_sem.at[2 + 2 * level + side]
            )
            copy.start()
            kept.append(copy)

    kept = []

    def squares_of(ref, start):
        def one(t, total):
            values = ref[pl.ds(pl.multiple_of(start + t * 256, 256), 256), :].astype(F32)
            return total + fold(values * values)

        return lax.fori_loop(0, 4, one, jnp.zeros((8, B), F32))

    spread(0, lax.rem(s, 2), D)
    scales = []
    for level in range(LEVELS):
        group, w, c = GROUP[level], WIDTH[level], COLUMN[level]
        block = 2 * D // group
        await_bytes(A[level].at[0 : (group - 1) * block], fr.at[level])
        share_rows(level)
        left = factor_of(squares_of(A[level], 0))
        right = factor_of(squares_of(A[level], D))
        scales.append((left, right))
        me = lax.rem(s, GROUP[level + 1])
        size = min(w, 256)
        for t in range(w // size):
            rows = slice(c + t * size, c + (t + 1) * size)
            ul = nn(WT[0, rows, :], A[level][0:D, :]) * left
            ur = nn(WT[1, rows, :], A[level][D : 2 * D, :]) * right
            joined = (1.0 + ul) * (1.0 + ur)
            UL[rows, :] = ul
            UR[rows, :] = ur
            JJ[rows, :] = joined
            A[level + 1][pl.ds(pl.multiple_of(me * w + t * size, size), size), :] = joined.astype(BF)
        spread(level + 1, me, w)

    def share_grads(level):
        w, c = WIDTH[level], COLUMN[level]
        ref = GX.at[:, c : c + w, at(p, B)]

        def one(i, carry):
            to_rep(ref, ref, gxs.at[level], gxr.at[level], lax.rem(p + i, REPS))
            return carry

        lax.fori_loop(1, REPS, one, 0)

    own = at(p, B)

    def scatter(level, me):
        group = GROUP[level]

        def one(i, carry):
            d = lax.rem(me + i, group)
            to_sub(BS[level].at[d], BR[level].at[me], bs.at[level], br.at[level], s - me + d)
            return carry

        lax.fori_loop(1, group, one, 0)
        copy = pltpu.make_async_copy(BS[level].at[me], BR[level].at[me], local_sem.at[14 + level])
        copy.start()
        return copy

    await_bytes(A5.at[0 : 31 * 32], fr.at[5])
    share_rows(5)
    root_scale = factor_of(squares_of(A5, 0))
    w, c = WIDTH[5], COLUMN[5]
    za = nn(WT[0, c:D, :], A5[...]) * root_scale
    zb = nn(WT[1, c:D, :], A5[...]) * root_scale
    sigma = 1.0 / (1.0 + jnp.exp(-zb))
    loads[4].wait()
    cotangent = COT[...].T
    ga = cotangent * sigma
    gb = cotangent * za * sigma * (1.0 - sigma)
    GX[0, c:D, own] = (ga * root_scale).astype(BF)
    GX[1, c:D, own] = (gb * root_scale).astype(BF)
    share_grads(5)
    ga = ga.astype(BF)
    gb = gb.astype(BF)
    GP[2, 0, 96:128, :] = ga
    GP[2, 1, 96:128, :] = gb
    dots = column_sum(ga.astype(F32) * za + gb.astype(F32) * zb)
    BS5[:, 32:48, :] = jnp.broadcast_to(split_tile(dots)[None], (SUBS, 16, B))

    def root_part(t, carry):
        rows = at(t, 256)
        part = nn(WN[0, rows, 896:1024], GP[2, 0]) + nn(WN[1, rows, 896:1024], GP[2, 1])
        BS5[at(t, 8), 0:32, :] = part.astype(BF).reshape(8, 32, B)
        return carry

    lax.fori_loop(0, 4, root_part, 0)
    own_chunk = scatter(5, s)

    def gathered(level, rows):
        group = GROUP[level]
        if group <= 8:
            total = BR[level][0, rows, :].astype(F32)
            for g in range(1, group):
                total = total + BR[level][g, rows, :].astype(F32)
            return total

        def one(i, total):
            for g in range(4):
                total = total + BR[level][4 * i + g, rows, :].astype(F32)
            return total

        size = rows.size if hasattr(rows, "size") else rows.stop - rows.start
        return lax.fori_loop(0, group // 4, one, jnp.zeros((size, B), F32))

    def await_chunks(level, copy):
        copy.wait()
        await_bytes(BR[level].at[0 : GROUP[level] - 1], br.at[level])
        size = CHUNK[level]
        return column_sum(gathered(level, slice(size, size + 16))) * (1.0 / D)

    for level in reversed(range(LEVELS)):
        group, w, c = GROUP[level], WIDTH[level], COLUMN[level]
        mean = await_chunks(level + 1, own_chunk)
        if level == LEVELS - 1:
            r = root_scale
        else:
            side_of = lax.rem(s // GROUP[level], 2)
            r = jnp.where(side_of == 1, scales[level + 1][1], scales[level + 1][0])
        left, right = scales[level]
        size = min(w, 64)

        def node_back(t, carry):
            dl, dr = carry
            rows = pl.ds(pl.multiple_of(c + t * size, size), size)
            total = gathered(level + 1, pl.ds(pl.multiple_of(t * size, size), size))
            ul, ur = UL[rows, :], UR[rows, :]
            v = r * (total - JJ[rows, :] * (r * mean))
            gl = v * (1.0 + ur)
            gr = v * (1.0 + ul)
            GX[0, rows, own] = (gl * left).astype(BF)
            GX[1, rows, own] = (gr * right).astype(BF)
            gl = gl.astype(BF)
            gr = gr.astype(BF)
            if level < 3:
                GB[0, rows, :] = gl
                GB[1, rows, :] = gr
            else:
                GP[level - 3, 0, c - 896 : c - 896 + w, :] = gl
                GP[level - 3, 1, c - 896 : c - 896 + w, :] = gr
            return dl + fold(gl.astype(F32) * ul), dr + fold(gr.astype(F32) * ur)

        zero = jnp.zeros((8, B), F32)
        dl, dr = lax.fori_loop(0, w // size, node_back, (zero, zero))
        half, chunk = group // 2, CHUNK[level]
        for side, dot in ((0, dl), (1, dr)):
            tile = split_tile(column_sum(dot))
            BS[level][side * half : (side + 1) * half, chunk : chunk + 16, :] = jnp.broadcast_to(
                tile[None], (half, 16, B)
            )

        def part(t, carry):
            rows = at(t, 256)
            for side in range(2):
                if level < 3:
                    value = nn(WN[side, rows, c : c + w], GB[side, c : c + w, :])
                else:
                    value = nn(WN[side, rows, 896:1024], GP[level - 3, side])
                value = value.astype(BF)
                if chunk >= 256:
                    per = chunk // 256
                    BS[level][side * half + t // per, at(lax.rem(t, per), 256), :] = value
                else:
                    n = 256 // chunk
                    BS[level][pl.ds(side * half + t * n, n), 0:chunk, :] = value.reshape(n, chunk, B)
            return carry

        lax.fori_loop(0, 4, part, 0)
        own_chunk = scatter(level, lax.rem(s, group))
        share_grads(level)

    mean = await_chunks(0, own_chunk)
    r = jnp.where(lax.rem(s, 2) == 1, scales[0][1], scales[0][0])

    def mid_back(t, carry):
        rows = at(t, 128)
        total = BR0[0, rows, :].astype(F32) + BR0[1, rows, :].astype(F32)
        v = r * (total - MP[rows, :] * (r * mean))
        rest = others([1.0 + MR[k, rows, :].astype(F32) for k in range(4)])
        for k in range(4):
            CS[k, rows, :] = (v * rest[k]).astype(BF)
        return carry

    lax.fori_loop(0, 8, mid_back, 0)

    def send_back(i, carry):
        peer = lax.rem(p + i, REPS)
        to_rep(CS.at[peer], CR.at[:, own], x3s, x3r.at[p], peer)
        return carry

    lax.fori_loop(1, REPS, send_back, 0)
    own_back = pltpu.make_async_copy(CS.at[p], CR.at[:, own], local_sem.at[20])
    own_back.start()

    for copy in kept:
        copy.wait()
    for level in range(LEVELS + 1):
        sides = 2 if level < LEVELS else 1
        for side in range(sides):
            await_bytes(AX.at[level, side, :, 0 : 3 * B], axr.at[level]) if sides == 1 else None
        if sides == 2:
            await_bytes(AX.at[level, :, :, 0 : 3 * B], axr.at[level])

    def await_grads(level):
        w, c = WIDTH[level], COLUMN[level]
        await_bytes(GX.at[:, c : c + w, 0 : 3 * B], gxr.at[level])

    for level in (5, 4, 3):
        await_grads(level)
    lane = lax.broadcasted_iota(jnp.int32, (256, 128), 1)
    for side in range(2):
        grads = GX[side, 896:1024, :]
        g3 = nt(AX[3, side], grads)
        g4 = nt(AX[4, side], grads)
        g5 = nt(AX[5, 0], grads)
        OU[side, :, 896:1024] = jnp.where(lane < 64, g3, jnp.where(lane < 96, g4, g5)).astype(BF)

    def upper_gradient(level):
        await_grads(level)
        w, c = WIDTH[level], COLUMN[level]
        for side in range(2):
            OU[side, :, c : c + w] = nt(AX[level, side], GX[side, c : c + w, :]).astype(BF)

    upper_gradient(2)
    upper_gradient(1)

    def leaf_back(i):
        lanes = at(source(i), B)

        def product(t, total):
            rows = at(t, 256)
            value = nn(MW[rows, :], CR[:, lanes])
            LB[rows, :] = value
            return total + fold(value * LP[rows, lanes])

        mean = column_sum(lax.fori_loop(0, 4, product, jnp.zeros((8, B), F32))) * (1.0 / D)
        r = RL[0:1, lanes]

        def cotangents(t, carry):
            rows = at(t, 128)
            v = r * (LB[rows, :] - LP[rows, lanes] * mean)
            rest = others([FK[k, rows, lanes] for k in range(4)])
            for k in range(4):
                CT[k, rows, lanes] = (v * rest[k]).astype(BF)
            return carry

        lax.fori_loop(0, 8, cotangents, 0)

    own_back.wait()
    leaf_back(0)

    def other_back(i, carry):
        src = source(i)
        await_bytes(CR.at[:, at(src, B)], x3r.at[src])
        leaf_back(i)
        return carry

    lax.fori_loop(1, REPS, other_back, 0)

    def leaf_gradient(k, carry):
        LW[k] = nt(XT[k], CT[k]).astype(BF)
        return carry

    lax.fori_loop(0, 4, leaf_gradient, 0)
    out_leaf = pltpu.make_async_copy(LW, lg_hbm, out_sem.at[0])
    out_leaf.start()

    def mid_gradient(t, carry):
        rows = at(t, 256)
        MWT[rows, :] = nt(LM[rows, :], CR[...]).astype(BF)
        return carry

    lax.fori_loop(0, 4, mid_gradient, 0)
    out_mid = pltpu.make_async_copy(MWT, mg_hbm, out_sem.at[1])
    out_mid.start()

    upper_gradient(0)

    def weave(t, carry):
        rows = at(t, 64)
        for side in range(2):
            OI[rows, side, :] = OU[side, rows, :]
        return carry

    lax.fori_loop(0, 4, weave, 0)
    out_upper = pltpu.make_async_copy(OI, ug_hbm, out_sem.at[2])
    out_upper.start()

    await_bytes(XS.at[0:3], x1s)
    await_bytes(MS.at[0:3], x2s)
    await_bytes(CS.at[0:3], x3s)
    for level in range(LEVELS + 1):
        group = GROUP[level]
        block = A[level].shape[0] // group
        await_bytes(A[level].at[0 : (group - 1) * block], fs.at[level])
        await_bytes(BS[level].at[0 : group - 1], bs.at[level])
        if level < LEVELS:
            await_bytes(AX.at[level, :, :, 0 : 3 * B], axs.at[level])
        else:
            await_bytes(AX.at[level, 0, :, 0 : 3 * B], axs.at[level])
        w, c = WIDTH[level], COLUMN[level]
        await_bytes(GX.at[:, c : c + w, 0 : 3 * B], gxs.at[level])
    out_leaf.wait()
    out_mid.wait()
    out_upper.wait()


def scratch():
    vm = pltpu.VMEM
    dma = pltpu.SemaphoreType.DMA
    chunks = [vm((GROUP[j], CHUNK[j] + 16, B), BF) for j in range(LEVELS + 1)]
    return (
        [
            vm((2048, F), BF), vm((256, 256), BF), vm((4, 4, B, F), BF), vm((4, ALL, F), BF),
            vm((4, F, D), BF), vm((4, D, F), BF), vm((D, D), BF), vm((D, D), BF),
            vm((D, 2, D), BF), vm((2, D, D), BF), vm((2, D, D), BF), vm((B, 32), F32),
            vm((4, D, ALL), F32), vm((D, ALL), F32), vm((8, ALL), F32), vm((D, ALL), BF),
            vm((4, D, B), BF), vm((4, D, B), BF), vm((D, B), F32),
        ]
        + [vm((2 * D, B), BF)] * 5
        + [vm((D, B), BF)]
        + [vm((D, B), F32)] * 3
        + [vm((3, 2, 128, B), BF), vm((2, D, B), BF)]
        + chunks
        + chunks
        + [
            vm((2, D, ALL), BF), vm((6, 2, 256, ALL), BF), vm((4, D, B), BF), vm((D, ALL), BF),
            vm((D, B), F32), vm((4, D, ALL), BF), vm((4, F, ALL), BF), vm((2, 256, D), BF),
            vm((256, 2, D), BF),
        ]
        + [
            dma((5,)), dma((21,)), dma, dma((4,)), dma, dma, dma, dma((4,)),
            dma((6,)), dma((6,)), dma((6,)), dma((6,)), dma((6,)), dma((6,)), dma((6,)), dma((6,)),
            dma((3,)),
        ]
    )


def on_device(regions, leaf_map, leaf_bond_weight, mid_weight, upper_weight, head_cotangent):
    anywhere = pl.BlockSpec(memory_space=pl.ANY)
    outs = pl.pallas_call(
        kernel,
        out_shape=(
            jax.ShapeDtypeStruct((4, F, D), BF),
            jax.ShapeDtypeStruct((D, D), BF),
            jax.ShapeDtypeStruct((256, 2, D), BF),
        ),
        in_specs=[pl.BlockSpec(memory_space=pltpu.SMEM)] + [anywhere] * 5,
        out_specs=(anywhere,) * 3,
        scratch_shapes=scratch(),
        compiler_params=pltpu.CompilerParams(
            collective_id=0, has_side_effects=True, vmem_limit_bytes=67000000
        ),
    )(
        leaf_map, regions.reshape(B * 16, F), leaf_bond_weight[0], mid_weight[0, 0],
        upper_weight[0], head_cotangent,
    )
    return (outs[0][None], outs[1][None, None], outs[2][None])


def solution(mesh):
    placed = (
        P("rep", "sub", None),
        P("sub"),
        P(("sub", "rep"), None, None, None),
        P("sub", "rep", None, None),
        P("sub", None, None, None),
        P("rep", "sub"),
    )
    return jax.shard_map(
        on_device,
        mesh=mesh,
        in_specs=placed,
        out_specs=(
            P(("sub", "rep"), None, None, None),
            P("sub", "rep", None, None),
            P("sub", "rep", None, None),
        ),
        check_vma=False,
    )
```

time: 565 us -> 180 us (0.32); the launches traced: 555 us -> 180 us
  waiting for transfers between devices: 312 us -> 0 us
  Pallas kernels: 0 us -> 171 us
  starting transfers between devices: 73.9 us -> 0 us
  matrix products: 51.2 us -> 0 us
  other arithmetic: 41.3 us -> 0 us
  blocking collectives: 34.7 us -> 0 us
  local copies, waits for them, and re-layouts: 26.1 us -> 7.61 us
  between operations: 15.4 us -> 0.65 us
    ppermute x35 -> x0, waiting for transfers between devices: 177 us -> none  [partner(): lax.ppermute(value, axis, [(i, i ^ 1 << bit) for i in range(lax.axis_size...]
    pallas_call x0 -> x1, Pallas kernels: none -> 171 us  [on_device(): pl.pallas_call(kernel, out_shape=(jax.ShapeDtypeStruct((4, F, D), BF), ja...]
    psum x1 -> x0, waiting for transfers between devices: 107 us -> none  [on_device(): lax.psum(root_term.astype(jnp.bfloat16), 'sub').astype(jnp.float32)]
    ppermute x35 -> x0, starting transfers between devices: 69.9 us -> none  [partner(): lax.ppermute(value, axis, [(i, i ^ 1 << bit) for i in range(lax.axis_size...]
    dot_general x35 -> x0, matrix products: 51.2 us -> none  [the longest x13 19.4 us: matmul_t(): lax.dot_general(left_arr, right_arr, (((1,), (1,)), ((), ())), preferred_...]
    all_to_all x2 -> x0, blocking collectives: 34.7 us -> none  [the longest x1 18.9 us: on_device(): lax.all_to_all(placed, 'rep', split_axis=1, concat_axis=0, tiled=True)[:, 0]]
    all_to_all x1 -> x0, waiting for transfers between devices: 18.8 us -> none  [on_device(): lax.all_to_all(middle_gradient_list, 'rep', split_axis=1, concat_axis=0,...]
    unnamed x113 -> x8, local copies, waits for them, and re-layouts: 20.4 us -> 7.61 us
  transfers between devices with their start and end apart: 38 -> 0, of which waited for: 37 -> 0; matrix products, arithmetic and copies ran while one was open for 6% -> 0% of each run, Pallas kernels for 0% -> 0%
where the time goes in v1:
time: 180 us
  Pallas kernels  171 us (95%)
  local copies, waits for them, and re-layouts  7.61 us (4%)
    pallas_call x1, Pallas kernels, on_device(): pl.pallas_call(kernel, out_shape=(jax.ShapeDtypeStruct((4, F, D), BF), ja...  171 us
    unnamed x8, local copies, waits for them, and re-layouts  7.61 us

profile of v1, /device:TPU:1, one launch (start us, length us, event | category | flops | bytes accessed | tf_op | source)
XLA Modules:
  0.0 179.6 jit_solution(8029912646572824986)
XLA Ops:
  0.6 1.4 copy.9.cot_hbm
  2.1 171.4 %shard_map.85 = (bf16[4,256,1024]{2,1,0:T(8,128)(2,1)}, bf16[1024,1024]{1,0:T(8,128)(2,1)}, bf16[256,2,1024]{2,1,0:T(2,128)(2,1)}) custom-call(s32[16]{0:T(128)} %map_ref.1, bf16[2048,256]{1,0:T(8,128)(2,1)} %bitcast.12, bf16[4,256,1024]{2,1,0:T(8,128)(2,1)} %bitcast.8, bf16[1024,1024]{1,0:T(8,128)(2,1)} %bitcast.9, bf16[1024,2,1024]{2,1,0:T(2,128)(2,1)} %bitcast.7, ...), custom_call_target="tpu_custom_call" | custom-call | tf_op jit(solution)/shard_map/pallas_call | solution.py:615
  173.4 0.0 copy-start
  173.5 3.2 %copy.13 = bf16[1,4,256,1024]{3,2,1,0:T(8,128)(2,1)} copy(bf16[1,4,256,1024]{3,2,1,0:T(8,128)(2,1)} %bitcast.11) | data formatting | bytes 4194304
  176.7 0.0 copy-done
  176.7 0.0 copy-start.1
  176.7 1.3 copy.14
  178.0 0.6 copy-done.1
  178.6 1.0 copy.15
Async XLA Ops:
  173.4 3.2 %copy-start = (bf16[1024,1024]{1,0:T(8,128)(2,1)S(1)}, bf16[1024,1024]{1,0:T(8,128)(2,1)}, u32[]{:S(2)}) copy-start(bf16[1024,1024]{1,0:T(8,128)(2,1)} %get-tuple-element.7) | copy-start | bytes 6291460
  176.7 2.0 %copy-start.1 = (bf16[256,2,1024]{2,1,0:T(2,128)(2,1)S(1)}, bf16[256,2,1024]{2,1,0:T(2,128)(2,1)}, u32[]{:S(2)}) copy-start(bf16[256,2,1024]{2,1,0:T(2,128)(2,1)} %get-tuple-element.8) | copy-start | bytes 3145732

commit v2 on v1

--- a/solution.py
+++ b/solution.py
@@ -62,15 +62,16 @@
 def kernel(
     map_ref, reg_hbm, lw_hbm, mw_hbm, uw_hbm, cot_hbm,
     lg_hbm, mg_hbm, ug_hbm,
-    R, Q, XS, XR, LW, LWT, MW, MWT, UW, WN, WT, COT, FK, LP, RL, LM, MS, MR, MP,
+    R, Q, XS, XR, LW, LWT, MW, MWT, UW, WN, WT, COT, FK, RL, LM, MS, MR,
     A0, A1, A2, A3, A4, A5, UL, UR, JJ, GP, GB,
-    BS0, BS1, BS2, BS3, BS4, BS5, BR0, BR1, BR2, BR3, BR4, BR5,
-    GX, AX, CS, CR, LB, CT, XT, OU, OI,
-    load_sem, local_sem, x1s, x1r, x2s, x2r, x3s, x3r, fs, fr, bs, br, axs, axr, gxs, gxr, out_sem,
+    BS1, BS2, BS3, BS4, BS5, BR1, BR2, BR3, BR4, BR5,
+    GX, AX, CS, CR, LB, CT, XT, OU, OI, LO, H0, R0, PR, PM,
+    load_sem, local_sem, x1s, x1r, x2s, x2r, x3s, x3r, h0s, h0r, fs, fr, ff, fo, bs, br,
+    axs, axr, gxs, gxr, gx0, pss, prs, out_sem,
 ):
     A = [A0, A1, A2, A3, A4, A5]
-    BS = [BS0, BS1, BS2, BS3, BS4, BS5]
-    BR = [BR0, BR1, BR2, BR3, BR4, BR5]
+    BS = [None, BS1, BS2, BS3, BS4, BS5]
+    BR = [None, BR1, BR2, BR3, BR4, BR5]
     s = lax.axis_index("sub")
     p = lax.axis_index("rep")
 
@@ -131,8 +132,11 @@
     lax.fori_loop(0, 8, place, 0)
     pl.semaphore_wait(barrier, SUBS - 1 + REPS - 1)
 
+    def source(i):
+        return lax.rem(p + i + i // 2 - 2 * (i // 3), REPS)
+
     def send_slots(i, carry):
-        peer = lax.rem(p + i, REPS)
+        peer = source(i)
         to_rep(XS.at[peer], XR.at[:, at(p, B), :], x1s, x1r.at[p], peer)
         return carry
 
@@ -157,9 +161,6 @@
         return carry
 
     lax.fori_loop(0, 16, turn_mid, 0)
-
-    def source(i):
-        return lax.rem(p + i + i // 2 - 2 * (i // 3), REPS)
 
     def leaf_chunk(i):
         src = source(i)
@@ -172,7 +173,7 @@
                 factor = 1.0 + nt(LWT[k, rows, :], XR[k, lanes, :])
                 FK[k, rows, lanes] = factor
                 product = factor if product is None else product * factor
-            LP[rows, lanes] = product
+            LB[rows, :] = product
             return squares + fold(product * product)
 
         r = factor_of(lax.fori_loop(0, 4, terms, jnp.zeros((8, B), F32)))
@@ -180,9 +181,7 @@
 
         def scale(t, carry):
             rows = at(t, 256)
-            h = LP[rows, lanes] * r
-            LP[rows, lanes] = h
-            LM[rows, lanes] = h.astype(BF)
+            LM[rows, lanes] = (LB[rows, :] * r).astype(BF)
             return carry
 
         lax.fori_loop(0, 4, scale, 0)
@@ -205,12 +204,16 @@
     own_mid.start()
     loads[3].wait()
 
+    def part_sides(t, carry):
+        WN[:, at(t, 32), :] = jnp.swapaxes(UW[at(t, 32)], 0, 1)
+        return carry
+
+    lax.fori_loop(0, 32, part_sides, 0)
+
     def turn_upper(t, carry):
         rows = at(t, 128)
         for side in range(2):
-            block = UW[rows, side, :]
-            WN[side, rows, :] = block
-            WT[side, :, rows] = block.T
+            WT[side, :, rows] = WN[side, rows, :].T
         return carry
 
     lax.fori_loop(0, 8, turn_upper, 0)
@@ -228,49 +231,65 @@
 
     own_mid.wait()
     await_bytes(MR.at[0:3], x2r)
-    base = lax.rem(s, 2) * D
+    c = lax.rem(s, 2)
+    partner = s + 1 - 2 * c
 
     def mid_product(t, carry):
         rows = at(t, 128)
         product = 1.0 + MR[0, rows, :].astype(F32)
         for k in range(1, 4):
             product = product * (1.0 + MR[k, rows, :].astype(F32))
-        MP[rows, :] = product
-        A0[pl.ds(pl.multiple_of(base + t * 128, 128), 128), :] = product.astype(BF)
+        A0[pl.ds(pl.multiple_of(c * D + t * 128, 128), 128), :] = product.astype(BF)
         return carry
 
     lax.fori_loop(0, 8, mid_product, 0)
 
+    own = at(p, B)
+
     def spread(level, me, block):
-        group = GROUP[level]
+        ref = A[level].at[at(me, block), :]
+        to_sub(ref, ref, fs.at[level], fo.at[level], partner)
 
         def one(i, carry):
-            peer = s - me + lax.rem(me + i, group)
-            ref = A[level].at[at(me, block), :]
-            to_sub(ref, ref, fs.at[level], fr.at[level], peer)
-            return carry
-
-        lax.fori_loop(1, group, one, 0)
+            peer = s - me + lax.rem(me + 2 * i, GROUP[level])
+            to_sub(ref, ref, fs.at[level], fr.at[level, i], peer)
+            return carry
+
+        if GROUP[level] > 2:
+            lax.fori_loop(1, GROUP[level] // 2, one, 0)
+
+    def collect(level, me, block):
+        half = GROUP[level] // 2
+
+        def one(i, carry):
+            ref = A[level].at[at(lax.rem(me - 2 * i + GROUP[level], GROUP[level]), block), :]
+            await_bytes(ref, fr.at[level, i])
+            to_sub(ref, ref, ff.at[level], fo.at[level], partner)
+            return carry
+
+        if half > 1:
+            lax.fori_loop(1, half, one, 0)
+        await_bytes(A[level].at[0 : half * block], fo.at[level])
 
     def share_rows(level):
-        sides = 2 if level < LEVELS else 1
+        sides = 2 if 0 < level < LEVELS else 1
+
+        def place_of(side, peer):
+            first = 1 - c if level == 0 else side
+            rows = pl.ds(pl.multiple_of(first * D + peer * 256, 256), 256)
+            return A[level].at[rows, :], AX.at[level, first, :, own]
 
         def one(i, carry):
-            peer = lax.rem(p + i, REPS)
+            peer = source(i)
             for side in range(sides):
-                rows = pl.ds(pl.multiple_of(side * D + peer * 256, 256), 256)
-                to_rep(
-                    A[level].at[rows, :], AX.at[level, side, :, at(p, B)],
-                    axs.at[level], axr.at[level], peer,
-                )
+                src, dst = place_of(side, peer)
+                to_rep(src, dst, axs.at[level], axr.at[level], peer)
             return carry
 
         lax.fori_loop(1, REPS, one, 0)
         for side in range(sides):
-            rows = pl.ds(pl.multiple_of(side * D + p * 256, 256), 256)
-            copy = pltpu.make_async_copy(
-                A[level].at[rows, :], AX.at[level, side, :, at(p, B)], local_sem.at[2 + 2 * level + side]
-            )
+            src, dst = place_of(side, p)
+            copy = pltpu.make_async_copy(src, dst, local_sem.at[2 + 2 * level + side])
             copy.start()
             kept.append(copy)
 
@@ -283,12 +302,39 @@
 
         return lax.fori_loop(0, 4, one, jnp.zeros((8, B), F32))
 
-    spread(0, lax.rem(s, 2), D)
+    spread(0, c, D)
+    message = A0.at[at(c, D), :]
+
+    def send_message(i, carry):
+        to_rep(message, H0.at[:, own], h0s, h0r, source(i))
+        return carry
+
+    def leave_one(t, carry):
+        rows = at(t, 128)
+        rest = others([1.0 + MR[k, rows, :].astype(F32) for k in range(4)])
+        for k in range(4):
+            CS[k, rows, :] = rest[k].astype(BF)
+        return carry
+
+    lax.fori_loop(0, 8, leave_one, 0)
+
+    def send_rest(i, carry):
+        peer = source(i)
+        to_rep(CS.at[peer], LO.at[:, own], x3s, x3r, peer)
+        return carry
+
+    lax.fori_loop(1, REPS, send_message, 0)
+    lax.fori_loop(1, REPS, send_rest, 0)
+    for copy in (
+        pltpu.make_async_copy(CS.at[p], LO.at[:, own], local_sem.at[20]),
+        pltpu.make_async_copy(message, H0.at[:, own], local_sem.at[21]),
+    ):
+        copy.start()
+        kept.append(copy)
     scales = []
     for level in range(LEVELS):
-        group, w, c = GROUP[level], WIDTH[level], COLUMN[level]
-        block = 2 * D // group
-        await_bytes(A[level].at[0 : (group - 1) * block], fr.at[level])
+        group, w, col = GROUP[level], WIDTH[level], COLUMN[level]
+        collect(level, lax.rem(s, group), 2 * D // group)
         share_rows(level)
         left = factor_of(squares_of(A[level], 0))
         right = factor_of(squares_of(A[level], D))
@@ -296,7 +342,7 @@
         me = lax.rem(s, GROUP[level + 1])
         size = min(w, 256)
         for t in range(w // size):
-            rows = slice(c + t * size, c + (t + 1) * size)
+            rows = slice(col + t * size, col + (t + 1) * size)
             ul = nn(WT[0, rows, :], A[level][0:D, :]) * left
             ur = nn(WT[1, rows, :], A[level][D : 2 * D, :]) * right
             joined = (1.0 + ul) * (1.0 + ur)
@@ -307,16 +353,14 @@
         spread(level + 1, me, w)
 
     def share_grads(level):
-        w, c = WIDTH[level], COLUMN[level]
-        ref = GX.at[:, c : c + w, at(p, B)]
+        w, col = WIDTH[level], COLUMN[level]
+        ref = GX.at[:, col : col + w, own]
 
         def one(i, carry):
-            to_rep(ref, ref, gxs.at[level], gxr.at[level], lax.rem(p + i, REPS))
+            to_rep(ref, ref, gxs.at[level], gxr.at[level] if level else gx0.at[p], source(i))
             return carry
 
         lax.fori_loop(1, REPS, one, 0)
-
-    own = at(p, B)
 
     def scatter(level, me):
         group = GROUP[level]
@@ -331,19 +375,19 @@
         copy.start()
         return copy
 
-    await_bytes(A5.at[0 : 31 * 32], fr.at[5])
+    collect(5, s, 32)
     share_rows(5)
     root_scale = factor_of(squares_of(A5, 0))
-    w, c = WIDTH[5], COLUMN[5]
-    za = nn(WT[0, c:D, :], A5[...]) * root_scale
-    zb = nn(WT[1, c:D, :], A5[...]) * root_scale
+    col = COLUMN[5]
+    za = nn(WT[0, col:D, :], A5[...]) * root_scale
+    zb = nn(WT[1, col:D, :], A5[...]) * root_scale
     sigma = 1.0 / (1.0 + jnp.exp(-zb))
     loads[4].wait()
-    cotangent = COT[...].T
+    cotangent = COT[...]
     ga = cotangent * sigma
     gb = cotangent * za * sigma * (1.0 - sigma)
-    GX[0, c:D, own] = (ga * root_scale).astype(BF)
-    GX[1, c:D, own] = (gb * root_scale).astype(BF)
+    GX[0, col:D, own] = (ga * root_scale).astype(BF)
+    GX[1, col:D, own] = (gb * root_scale).astype(BF)
     share_grads(5)
     ga = ga.astype(BF)
     gb = gb.astype(BF)
@@ -384,7 +428,7 @@
         return column_sum(gathered(level, slice(size, size + 16))) * (1.0 / D)
 
     for level in reversed(range(LEVELS)):
-        group, w, c = GROUP[level], WIDTH[level], COLUMN[level]
+        group, w, col = GROUP[level], WIDTH[level], COLUMN[level]
         mean = await_chunks(level + 1, own_chunk)
         if level == LEVELS - 1:
             r = root_scale
@@ -396,7 +440,7 @@
 
         def node_back(t, carry):
             dl, dr = carry
-            rows = pl.ds(pl.multiple_of(c + t * size, size), size)
+            rows = pl.ds(pl.multiple_of(col + t * size, size), size)
             total = gathered(level + 1, pl.ds(pl.multiple_of(t * size, size), size))
             ul, ur = UL[rows, :], UR[rows, :]
             v = r * (total - JJ[rows, :] * (r * mean))
@@ -404,18 +448,23 @@
             gr = v * (1.0 + ul)
             GX[0, rows, own] = (gl * left).astype(BF)
             GX[1, rows, own] = (gr * right).astype(BF)
+            if level == 0:
+                return carry
             gl = gl.astype(BF)
             gr = gr.astype(BF)
             if level < 3:
                 GB[0, rows, :] = gl
                 GB[1, rows, :] = gr
             else:
-                GP[level - 3, 0, c - 896 : c - 896 + w, :] = gl
-                GP[level - 3, 1, c - 896 : c - 896 + w, :] = gr
+                GP[level - 3, 0, col - 896 : col - 896 + w, :] = gl
+                GP[level - 3, 1, col - 896 : col - 896 + w, :] = gr
             return dl + fold(gl.astype(F32) * ul), dr + fold(gr.astype(F32) * ur)
 
         zero = jnp.zeros((8, B), F32)
         dl, dr = lax.fori_loop(0, w // size, node_back, (zero, zero))
+        if level == 0:
+            share_grads(0)
+            break
         half, chunk = group // 2, CHUNK[level]
         for side, dot in ((0, dl), (1, dr)):
             tile = split_tile(column_sum(dot))
@@ -427,7 +476,7 @@
             rows = at(t, 256)
             for side in range(2):
                 if level < 3:
-                    value = nn(WN[side, rows, c : c + w], GB[side, c : c + w, :])
+                    value = nn(WN[side, rows, col : col + w], GB[side, col : col + w, :])
                 else:
                     value = nn(WN[side, rows, 896:1024], GP[level - 3, side])
                 value = value.astype(BF)
@@ -443,41 +492,52 @@
         own_chunk = scatter(level, lax.rem(s, group))
         share_grads(level)
 
-    mean = await_chunks(0, own_chunk)
-    r = jnp.where(lax.rem(s, 2) == 1, scales[0][1], scales[0][0])
-
-    def mid_back(t, carry):
-        rows = at(t, 128)
-        total = BR0[0, rows, :].astype(F32) + BR0[1, rows, :].astype(F32)
-        v = r * (total - MP[rows, :] * (r * mean))
-        rest = others([1.0 + MR[k, rows, :].astype(F32) for k in range(4)])
-        for k in range(4):
-            CS[k, rows, :] = (v * rest[k]).astype(BF)
-        return carry
-
-    lax.fori_loop(0, 8, mid_back, 0)
-
-    def send_back(i, carry):
-        peer = lax.rem(p + i, REPS)
-        to_rep(CS.at[peer], CR.at[:, own], x3s, x3r.at[p], peer)
-        return carry
-
-    lax.fori_loop(1, REPS, send_back, 0)
-    own_back = pltpu.make_async_copy(CS.at[p], CR.at[:, own], local_sem.at[20])
-    own_back.start()
+    await_bytes(MS.at[0:3], x2s)
+
+    def partial_sums(i):
+        src = source(i)
+        slot = i // 2 - i // 3
+        lanes = at(src, B)
+        if i:
+            await_bytes(GX.at[:, 0:512, lanes], gx0.at[src])
+
+        def other(t, carry):
+            rows = at(t, 256)
+            MS[src, rows, :] = nn(WN[1 - c, rows, 0:512], GX[1 - c, 0:512, lanes]).astype(BF)
+            return carry
+
+        def mine(t, carry):
+            rows = at(t, 256)
+            PM[slot, rows, :] = nn(WN[c, rows, 0:512], GX[c, 0:512, lanes])
+            return carry
+
+        lax.fori_loop(0, 4, other, 0)
+        to_sub(MS.at[src], PR.at[src], pss, prs.at[src], partner)
+        lax.fori_loop(0, 4, mine, 0)
+
+    partial_sums(0)
 
     for copy in kept:
         copy.wait()
     for level in range(LEVELS + 1):
-        sides = 2 if level < LEVELS else 1
-        for side in range(sides):
-            await_bytes(AX.at[level, side, :, 0 : 3 * B], axr.at[level]) if sides == 1 else None
-        if sides == 2:
+        if 0 < level < LEVELS:
             await_bytes(AX.at[level, :, :, 0 : 3 * B], axr.at[level])
+        else:
+            await_bytes(AX.at[level, 0, :, 0 : 3 * B], axr.at[level])
+    await_bytes(LO.at[:, 0 : 3 * B], x3r)
+    await_bytes(H0.at[:, 0 : 3 * B], h0r)
+
+    def message_scale(t, total):
+        values = H0[at(t, 128), :].astype(F32)
+        return total + fold(values * values)
+
+    R0[...] = jnp.broadcast_to(
+        factor_of(lax.fori_loop(0, 8, message_scale, jnp.zeros((8, ALL), F32))), (8, ALL)
+    )
 
     def await_grads(level):
-        w, c = WIDTH[level], COLUMN[level]
-        await_bytes(GX.at[:, c : c + w, 0 : 3 * B], gxr.at[level])
+        w, col = WIDTH[level], COLUMN[level]
+        await_bytes(GX.at[:, col : col + w, 0 : 3 * B], gxr.at[level])
 
     for level in (5, 4, 3):
         await_grads(level)
@@ -489,30 +549,48 @@
         g5 = nt(AX[5, 0], grads)
         OU[side, :, 896:1024] = jnp.where(lane < 64, g3, jnp.where(lane < 96, g4, g5)).astype(BF)
 
-    def upper_gradient(level):
+    for level in (2, 1):
         await_grads(level)
-        w, c = WIDTH[level], COLUMN[level]
+        w, col = WIDTH[level], COLUMN[level]
         for side in range(2):
-            OU[side, :, c : c + w] = nt(AX[level, side], GX[side, c : c + w, :]).astype(BF)
-
-    upper_gradient(2)
-    upper_gradient(1)
+            OU[side, :, col : col + w] = nt(AX[level, side], GX[side, col : col + w, :]).astype(BF)
 
     def leaf_back(i):
-        lanes = at(source(i), B)
+        src = source(i)
+        slot = i // 2 - i // 3
+        lanes = at(src, B)
+        await_bytes(PR.at[src], prs.at[src])
+        scale0 = R0[0:1, lanes]
+
+        def add_parts(t, total):
+            rows = at(t, 128)
+            value = PM[slot, rows, :] + PR[src, rows, :].astype(F32)
+            PM[slot, rows, :] = value
+            return total + fold(value * H0[rows, lanes].astype(F32))
+
+        mean0 = column_sum(lax.fori_loop(0, 8, add_parts, jnp.zeros((8, B), F32))) * (1.0 / D)
+        shift = scale0 * scale0 * mean0
+
+        def mid_back(t, carry):
+            rows = at(t, 128)
+            v = PM[slot, rows, :] - H0[rows, lanes].astype(F32) * shift
+            CR[rows, lanes] = (v * LO[rows, lanes].astype(F32)).astype(BF)
+            return carry
+
+        lax.fori_loop(0, 8, mid_back, 0)
 
         def product(t, total):
             rows = at(t, 256)
             value = nn(MW[rows, :], CR[:, lanes])
             LB[rows, :] = value
-            return total + fold(value * LP[rows, lanes])
+            return total + fold(value * LM[rows, lanes].astype(F32))
 
         mean = column_sum(lax.fori_loop(0, 4, product, jnp.zeros((8, B), F32))) * (1.0 / D)
         r = RL[0:1, lanes]
 
         def cotangents(t, carry):
             rows = at(t, 128)
-            v = r * (LB[rows, :] - LP[rows, lanes] * mean)
+            v = r * (LB[rows, :] - LM[rows, lanes].astype(F32) * mean)
             rest = others([FK[k, rows, lanes] for k in range(4)])
             for k in range(4):
                 CT[k, rows, lanes] = (v * rest[k]).astype(BF)
@@ -520,35 +598,16 @@
 
         lax.fori_loop(0, 8, cotangents, 0)
 
-    own_back.wait()
     leaf_back(0)
-
-    def other_back(i, carry):
-        src = source(i)
-        await_bytes(CR.at[:, at(src, B)], x3r.at[src])
-        leaf_back(i)
-        return carry
-
-    lax.fori_loop(1, REPS, other_back, 0)
-
-    def leaf_gradient(k, carry):
-        LW[k] = nt(XT[k], CT[k]).astype(BF)
-        return carry
-
-    lax.fori_loop(0, 4, leaf_gradient, 0)
-    out_leaf = pltpu.make_async_copy(LW, lg_hbm, out_sem.at[0])
-    out_leaf.start()
-
-    def mid_gradient(t, carry):
-        rows = at(t, 256)
-        MWT[rows, :] = nt(LM[rows, :], CR[...]).astype(BF)
-        return carry
-
-    lax.fori_loop(0, 4, mid_gradient, 0)
-    out_mid = pltpu.make_async_copy(MWT, mg_hbm, out_sem.at[1])
-    out_mid.start()
-
-    upper_gradient(0)
+    partial_sums(1)
+    partial_sums(2)
+    leaf_back(1)
+    leaf_back(2)
+    partial_sums(3)
+
+    rows = at(p, 256)
+    OU[c, :, 0:512] = nt(H0[rows, :], GX[c, 0:512, :]).astype(BF)
+    OU[1 - c, :, 0:512] = nt(AX[0, 1 - c], GX[1 - c, 0:512, :]).astype(BF)
 
     def weave(t, carry):
         rows = at(t, 64)
@@ -559,21 +618,43 @@
     lax.fori_loop(0, 4, weave, 0)
     out_upper = pltpu.make_async_copy(OI, ug_hbm, out_sem.at[2])
     out_upper.start()
+    leaf_back(3)
+
+    def leaf_gradient(k, carry):
+        LW[k] = nt(XT[k], CT[k]).astype(BF)
+        return carry
+
+    lax.fori_loop(0, 4, leaf_gradient, 0)
+    out_leaf = pltpu.make_async_copy(LW, lg_hbm, out_sem.at[0])
+    out_leaf.start()
+
+    def mid_gradient(t, carry):
+        rows = at(t, 256)
+        MWT[rows, :] = nt(LM[rows, :], CR[...]).astype(BF)
+        return carry
+
+    lax.fori_loop(0, 4, mid_gradient, 0)
+    out_mid = pltpu.make_async_copy(MWT, mg_hbm, out_sem.at[1])
+    out_mid.start()
 
     await_bytes(XS.at[0:3], x1s)
-    await_bytes(MS.at[0:3], x2s)
     await_bytes(CS.at[0:3], x3s)
+    await_bytes(H0.at[:, 0 : 3 * B], h0s)
+    await_bytes(MS, pss)
     for level in range(LEVELS + 1):
-        group = GROUP[level]
-        block = A[level].shape[0] // group
-        await_bytes(A[level].at[0 : (group - 1) * block], fs.at[level])
-        await_bytes(BS[level].at[0 : group - 1], bs.at[level])
-        if level < LEVELS:
+        half = GROUP[level] // 2
+        block = A[level].shape[0] // GROUP[level]
+        await_bytes(A[level].at[0 : half * block], fs.at[level])
+        if half > 1:
+            await_bytes(A[level].at[0 : (half - 1) * block], ff.at[level])
+        if level:
+            await_bytes(BS[level].at[0 : GROUP[level] - 1], bs.at[level])
+        if 0 < level < LEVELS:
             await_bytes(AX.at[level, :, :, 0 : 3 * B], axs.at[level])
         else:
             await_bytes(AX.at[level, 0, :, 0 : 3 * B], axs.at[level])
-        w, c = WIDTH[level], COLUMN[level]
-        await_bytes(GX.at[:, c : c + w, 0 : 3 * B], gxs.at[level])
+        w, col = WIDTH[level], COLUMN[level]
+        await_bytes(GX.at[:, col : col + w, 0 : 3 * B], gxs.at[level])
     out_leaf.wait()
     out_mid.wait()
     out_upper.wait()
@@ -582,14 +663,14 @@
 def scratch():
     vm = pltpu.VMEM
     dma = pltpu.SemaphoreType.DMA
-    chunks = [vm((GROUP[j], CHUNK[j] + 16, B), BF) for j in range(LEVELS + 1)]
+    chunks = [vm((GROUP[j], CHUNK[j] + 16, B), BF) for j in range(1, LEVELS + 1)]
     return (
         [
             vm((2048, F), BF), vm((256, 256), BF), vm((4, 4, B, F), BF), vm((4, ALL, F), BF),
             vm((4, F, D), BF), vm((4, D, F), BF), vm((D, D), BF), vm((D, D), BF),
-            vm((D, 2, D), BF), vm((2, D, D), BF), vm((2, D, D), BF), vm((B, 32), F32),
-            vm((4, D, ALL), F32), vm((D, ALL), F32), vm((8, ALL), F32), vm((D, ALL), BF),
-            vm((4, D, B), BF), vm((4, D, B), BF), vm((D, B), F32),
+            vm((D, 2, D), BF), vm((2, D, D), BF), vm((2, D, D), BF), vm((32, B), F32),
+            vm((4, D, ALL), F32), vm((8, ALL), F32), vm((D, ALL), BF),
+            vm((4, D, B), BF), vm((4, D, B), BF),
         ]
         + [vm((2 * D, B), BF)] * 5
         + [vm((D, B), BF)]
@@ -600,12 +681,13 @@
         + [
             vm((2, D, ALL), BF), vm((6, 2, 256, ALL), BF), vm((4, D, B), BF), vm((D, ALL), BF),
             vm((D, B), F32), vm((4, D, ALL), BF), vm((4, F, ALL), BF), vm((2, 256, D), BF),
-            vm((256, 2, D), BF),
+            vm((256, 2, D), BF), vm((D, ALL), BF), vm((D, ALL), BF), vm((8, ALL), F32),
+            vm((4, D, B), BF), vm((2, D, B), F32),
         ]
         + [
-            dma((5,)), dma((21,)), dma, dma((4,)), dma, dma, dma, dma((4,)),
-            dma((6,)), dma((6,)), dma((6,)), dma((6,)), dma((6,)), dma((6,)), dma((6,)), dma((6,)),
-            dma((3,)),
+            dma((5,)), dma((22,)), dma, dma((4,)), dma, dma, dma, dma, dma, dma,
+            dma((6,)), dma((6, 16)), dma((6,)), dma((6,)), dma((6,)), dma((6,)),
+            dma((6,)), dma((6,)), dma((6,)), dma((6,)), dma((4,)), dma, dma((4,)), dma((3,)),
         ]
     )
 
@@ -627,7 +709,7 @@
         ),
     )(
         leaf_map, regions.reshape(B * 16, F), leaf_bond_weight[0], mid_weight[0, 0],
-        upper_weight[0], head_cotangent,
+        upper_weight[0], head_cotangent.T,
     )
     return (outs[0][None], outs[1][None, None], outs[2][None])
 

time: 180 us -> 159 us (0.88)
  Pallas kernels: 171 us -> 152 us
    pallas_call x1, Pallas kernels: 171 us -> 152 us  [on_device(): pl.pallas_call(kernel, out_shape=(jax.ShapeDtypeStruct((4, F, D), BF), ja...]
    unnamed x8 -> x7, local copies, waits for them, and re-layouts: 7.61 us -> 6.16 us
where the time goes in v2:
time: 159 us
  Pallas kernels  152 us (96%)
  local copies, waits for them, and re-layouts  6.16 us (4%)
    pallas_call x1, Pallas kernels, on_device(): pl.pallas_call(kernel, out_shape=(jax.ShapeDtypeStruct((4, F, D), BF), ja...  152 us
    unnamed x7, local copies, waits for them, and re-layouts  6.16 us

profile of v2, /device:TPU:1, one launch (start us, length us, event | category | flops | bytes accessed | tf_op | source)
XLA Modules:
  0.0 158.8 jit_solution(3679106823480546530)
XLA Ops:
  0.6 152.0 %shard_map.85 = (bf16[4,256,1024]{2,1,0:T(8,128)(2,1)}, bf16[1024,1024]{1,0:T(8,128)(2,1)}, bf16[256,2,1024]{2,1,0:T(2,128)(2,1)}) custom-call(s32[16]{0:T(128)} %map_ref.1, bf16[2048,256]{1,0:T(8,128)(2,1)} %bitcast.13, bf16[4,256,1024]{2,1,0:T(8,128)(2,1)} %bitcast.9, bf16[1024,1024]{1,0:T(8,128)(2,1)} %bitcast.10, bf16[1024,2,1024]{2,1,0:T(2,128)(2,1)} %bitcast.8, ...), custom_call_target="tpu_custom_call" | custom-call | tf_op jit(solution)/shard_map/pallas_call | solution.py:697
  152.6 0.0 copy-start
  152.6 3.2 %copy.12 = bf16[1,4,256,1024]{3,2,1,0:T(8,128)(2,1)} copy(bf16[1,4,256,1024]{3,2,1,0:T(8,128)(2,1)} %bitcast.12) | data formatting | bytes 4194304
  155.8 0.0 copy-done
  155.8 0.0 copy-start.1
  155.8 1.3 copy.13
  157.2 0.6 copy-done.1
  157.8 1.0 copy.14
Async XLA Ops:
  152.6 3.2 %copy-start = (bf16[1024,1024]{1,0:T(8,128)(2,1)S(1)}, bf16[1024,1024]{1,0:T(8,128)(2,1)}, u32[]{:S(2)}) copy-start(bf16[1024,1024]{1,0:T(8,128)(2,1)} %get-tuple-element.7) | copy-start | bytes 6291460
  155.8 2.0 %copy-start.1 = (bf16[256,2,1024]{2,1,0:T(2,128)(2,1)S(1)}, bf16[256,2,1024]{2,1,0:T(2,128)(2,1)}, u32[]{:S(2)}) copy-start(bf16[256,2,1024]{2,1,0:T(2,128)(2,1)} %get-tuple-element.8) | copy-start | bytes 3145732

commit v3 on v2

--- a/solution.py
+++ b/solution.py
@@ -46,6 +46,14 @@
     return pl.ds(pl.multiple_of(index * size, size), size)
 
 
+def lanes_of(i):
+    return slice(i * B, (i + 1) * B)
+
+
+OFFSET = (0, 1, 3, 2)
+BACK = (0, 2, 1, 3)
+
+
 def others(f):
     p01 = f[0] * f[1]
     p23 = f[2] * f[3]
@@ -63,10 +71,10 @@
     map_ref, reg_hbm, lw_hbm, mw_hbm, uw_hbm, cot_hbm,
     lg_hbm, mg_hbm, ug_hbm,
     R, Q, XS, XR, LW, LWT, MW, MWT, UW, WN, WT, COT, FK, RL, LM, MS, MR,
-    A0, A1, A2, A3, A4, A5, UL, UR, JJ, GP, GB,
+    A0, A1, A2, A3, A4, A5, UL, UR, JJ, GP, GB, WP, BO, BI, PF,
     BS1, BS2, BS3, BS4, BS5, BR1, BR2, BR3, BR4, BR5,
     GX, AX, CS, CR, LB, CT, XT, OU, OI, LO, H0, R0, PR, PM,
-    load_sem, local_sem, x1s, x1r, x2s, x2r, x3s, x3r, h0s, h0r, fs, fr, ff, fo, bs, br,
+    load_sem, local_sem, x1s, x1r, x2s, x2r, x3s, x3r, h0s, h0r, fs, fr, ff, fo, bs, br, bos, bis,
     axs, axr, gxs, gxr, gx0, pss, prs, out_sem,
 ):
     A = [A0, A1, A2, A3, A4, A5]
@@ -133,15 +141,12 @@
     pl.semaphore_wait(barrier, SUBS - 1 + REPS - 1)
 
     def source(i):
-        return lax.rem(p + i + i // 2 - 2 * (i // 3), REPS)
-
-    def send_slots(i, carry):
+        return lax.rem(p + OFFSET[i], REPS)
+
+    for i in range(1, REPS):
         peer = source(i)
-        to_rep(XS.at[peer], XR.at[:, at(p, B), :], x1s, x1r.at[p], peer)
-        return carry
-
-    lax.fori_loop(1, REPS, send_slots, 0)
-    own_slots = pltpu.make_async_copy(XS.at[p], XR.at[:, at(p, B), :], local_sem.at[0])
+        to_rep(XS.at[peer], XR.at[:, lanes_of(BACK[i]), :], x1s, x1r.at[BACK[i]], peer)
+    own_slots = pltpu.make_async_copy(XS.at[p], XR.at[:, 0:B, :], local_sem.at[0])
     own_slots.start()
 
     GP[...] = jnp.zeros(GP.shape, BF)
@@ -162,45 +167,36 @@
 
     lax.fori_loop(0, 16, turn_mid, 0)
 
-    def leaf_chunk(i):
-        src = source(i)
-        lanes = at(src, B)
-
-        def terms(t, squares):
-            rows = at(t, 256)
+    def leaf_blocks(lanes):
+        n = lanes.stop - lanes.start
+        squares = jnp.zeros((8, n), F32)
+        for t in range(4):
+            rows = slice(256 * t, 256 * (t + 1))
             product = None
             for k in range(4):
                 factor = 1.0 + nt(LWT[k, rows, :], XR[k, lanes, :])
-                FK[k, rows, lanes] = factor
+                FK[k, rows, lanes] = factor.astype(BF)
                 product = factor if product is None else product * factor
-            LB[rows, :] = product
-            return squares + fold(product * product)
-
-        r = factor_of(lax.fori_loop(0, 4, terms, jnp.zeros((8, B), F32)))
-        RL[:, lanes] = jnp.broadcast_to(r, (8, B))
-
-        def scale(t, carry):
-            rows = at(t, 256)
-            LM[rows, lanes] = (LB[rows, :] * r).astype(BF)
-            return carry
-
-        lax.fori_loop(0, 4, scale, 0)
-
-        def mid(t, carry):
-            rows = at(t, 256)
-            MS[src, rows, :] = nn(MWT[rows, :], LM[:, lanes]).astype(BF)
-            return carry
-
-        lax.fori_loop(0, 4, mid, 0)
-
-    def turn_slots(i):
-        lanes = at(source(i), B)
+            LB[rows, 0:n] = product
+            squares = squares + fold(product * product)
+        r = factor_of(squares)
+        RL[:, lanes] = jnp.broadcast_to(r, (8, n))
+        for t in range(4):
+            rows = slice(256 * t, 256 * (t + 1))
+            LM[rows, lanes] = (LB[rows, 0:n] * r).astype(BF)
+        for t in range(4):
+            rows = slice(256 * t, 256 * (t + 1))
+            value = nn(MWT[rows, :], LM[:, lanes]).astype(BF)
+            for b in range(n // B):
+                MS[lanes.start // B + b, rows, :] = value[:, lanes_of(b)]
+
+    def turn_slots(lanes):
         for k in range(4):
             XT[k, :, lanes] = XR[k, lanes, :].T
 
     own_slots.wait()
-    leaf_chunk(0)
-    own_mid = pltpu.make_async_copy(MS.at[p], MR.at[p], local_sem.at[1])
+    leaf_blocks(slice(0, B))
+    own_mid = pltpu.make_async_copy(MS.at[0], MR.at[p], local_sem.at[1])
     own_mid.start()
     loads[3].wait()
 
@@ -217,34 +213,38 @@
         return carry
 
     lax.fori_loop(0, 8, turn_upper, 0)
-    turn_slots(0)
-
-    def other_chunk(i, carry):
-        src = source(i)
-        await_bytes(XR.at[:, at(src, B), :], x1r.at[src])
-        leaf_chunk(i)
-        to_rep(MS.at[src], MR.at[p], x2s, x2r, src)
-        turn_slots(i)
-        return carry
-
-    lax.fori_loop(1, REPS, other_chunk, 0)
+    for level in (2, 3, 4):
+        size = CHUNK[level]
+        col = min(COLUMN[level], 896)
+        count = D // size
+        for side in range(2):
+            for q in range(count):
+                to = (q % 2 * (count // 2) + q // 2) * size
+                WP[level - 2, side, to : to + size, :] = WN[side, q * size : (q + 1) * size, col : col + 128]
+    turn_slots(slice(0, B))
+
+    for blocks in ((1, 2), (3,)):
+        for i in blocks:
+            await_bytes(XR.at[:, lanes_of(i), :], x1r.at[i])
+        lanes = slice(blocks[0] * B, (blocks[-1] + 1) * B)
+        leaf_blocks(lanes)
+        for i in blocks:
+            to_rep(MS.at[i], MR.at[p], x2s, x2r, source(i))
+        turn_slots(lanes)
 
     own_mid.wait()
     await_bytes(MR.at[0:3], x2r)
     c = lax.rem(s, 2)
     partner = s + 1 - 2 * c
 
-    def mid_product(t, carry):
-        rows = at(t, 128)
+    for t in range(8):
+        rows = slice(128 * t, 128 * (t + 1))
         product = 1.0 + MR[0, rows, :].astype(F32)
         for k in range(1, 4):
             product = product * (1.0 + MR[k, rows, :].astype(F32))
         A0[pl.ds(pl.multiple_of(c * D + t * 128, 128), 128), :] = product.astype(BF)
-        return carry
-
-    lax.fori_loop(0, 8, mid_product, 0)
-
-    own = at(p, B)
+
+    own = slice(0, B)
 
     def spread(level, me, block):
         ref = A[level].at[at(me, block), :]
@@ -274,40 +274,32 @@
     def share_rows(level):
         sides = 2 if 0 < level < LEVELS else 1
 
-        def place_of(side, peer):
+        def place_of(side, i):
             first = 1 - c if level == 0 else side
-            rows = pl.ds(pl.multiple_of(first * D + peer * 256, 256), 256)
-            return A[level].at[rows, :], AX.at[level, first, :, own]
-
-        def one(i, carry):
-            peer = source(i)
+            rows = pl.ds(pl.multiple_of(first * D + source(i) * 256, 256), 256)
+            return A[level].at[rows, :], AX.at[level, first, :, lanes_of(BACK[i])]
+
+        for i in range(1, REPS):
             for side in range(sides):
-                src, dst = place_of(side, peer)
-                to_rep(src, dst, axs.at[level], axr.at[level], peer)
-            return carry
-
-        lax.fori_loop(1, REPS, one, 0)
+                src, dst = place_of(side, i)
+                to_rep(src, dst, axs.at[level], axr.at[level], source(i))
         for side in range(sides):
-            src, dst = place_of(side, p)
+            src, dst = place_of(side, 0)
             copy = pltpu.make_async_copy(src, dst, local_sem.at[2 + 2 * level + side])
             copy.start()
             kept.append(copy)
 
     kept = []
 
-    def squares_of(ref, start):
-        def one(t, total):
-            values = ref[pl.ds(pl.multiple_of(start + t * 256, 256), 256), :].astype(F32)
-            return total + fold(values * values)
-
-        return lax.fori_loop(0, 4, one, jnp.zeros((8, B), F32))
+    def squares_of(ref, start, lanes=slice(0, B)):
+        total = jnp.zeros((8, B), F32)
+        for t in range(4):
+            values = ref[start + 256 * t : start + 256 * (t + 1), lanes].astype(F32)
+            total = total + fold(values * values)
+        return total
 
     spread(0, c, D)
     message = A0.at[at(c, D), :]
-
-    def send_message(i, carry):
-        to_rep(message, H0.at[:, own], h0s, h0r, source(i))
-        return carry
 
     def leave_one(t, carry):
         rows = at(t, 128)
@@ -318,13 +310,10 @@
 
     lax.fori_loop(0, 8, leave_one, 0)
 
-    def send_rest(i, carry):
-        peer = source(i)
-        to_rep(CS.at[peer], LO.at[:, own], x3s, x3r, peer)
-        return carry
-
-    lax.fori_loop(1, REPS, send_message, 0)
-    lax.fori_loop(1, REPS, send_rest, 0)
+    for i in range(1, REPS):
+        to_rep(message, H0.at[:, lanes_of(BACK[i])], h0s, h0r, source(i))
+    for i in range(1, REPS):
+        to_rep(CS.at[source(i)], LO.at[:, lanes_of(BACK[i])], x3s, x3r, source(i))
     for copy in (
         pltpu.make_async_copy(CS.at[p], LO.at[:, own], local_sem.at[20]),
         pltpu.make_async_copy(message, H0.at[:, own], local_sem.at[21]),
@@ -354,24 +343,27 @@
 
     def share_grads(level):
         w, col = WIDTH[level], COLUMN[level]
-        ref = GX.at[:, col : col + w, own]
+        for i in range(1, REPS):
+            to_rep(
+                GX.at[:, col : col + w, own], GX.at[:, col : col + w, lanes_of(BACK[i])],
+                gxs.at[level], gxr.at[level] if level else gx0.at[BACK[i]], source(i),
+            )
+
+    def scatter(level, me):
+        chips = GROUP[level] // 2 if level < LEVELS else SUBS
+        step = 2 if level < LEVELS else 1
+        at_chip = me // step
 
         def one(i, carry):
-            to_rep(ref, ref, gxs.at[level], gxr.at[level] if level else gx0.at[p], source(i))
+            d = lax.rem(at_chip + i, chips)
+            peer = s + (d - at_chip) * step
+            to_sub(BS[level].at[d], BR[level].at[at_chip], bs.at[level], br.at[level], peer)
             return carry
 
-        lax.fori_loop(1, REPS, one, 0)
-
-    def scatter(level, me):
-        group = GROUP[level]
-
-        def one(i, carry):
-            d = lax.rem(me + i, group)
-            to_sub(BS[level].at[d], BR[level].at[me], bs.at[level], br.at[level], s - me + d)
-            return carry
-
-        lax.fori_loop(1, group, one, 0)
-        copy = pltpu.make_async_copy(BS[level].at[me], BR[level].at[me], local_sem.at[14 + level])
+        lax.fori_loop(1, chips, one, 0)
+        copy = pltpu.make_async_copy(
+            BS[level].at[at_chip], BR[level].at[at_chip], local_sem.at[14 + level]
+        )
         copy.start()
         return copy
 
@@ -396,34 +388,22 @@
     dots = column_sum(ga.astype(F32) * za + gb.astype(F32) * zb)
     BS5[:, 32:48, :] = jnp.broadcast_to(split_tile(dots)[None], (SUBS, 16, B))
 
-    def root_part(t, carry):
-        rows = at(t, 256)
+    for t in range(4):
+        rows = slice(256 * t, 256 * (t + 1))
         part = nn(WN[0, rows, 896:1024], GP[2, 0]) + nn(WN[1, rows, 896:1024], GP[2, 1])
-        BS5[at(t, 8), 0:32, :] = part.astype(BF).reshape(8, 32, B)
-        return carry
-
-    lax.fori_loop(0, 4, root_part, 0)
+        BS5[8 * t : 8 * t + 8, 0:32, :] = part.astype(BF).reshape(8, 32, B)
     own_chunk = scatter(5, s)
 
     def gathered(level, rows):
-        group = GROUP[level]
-        if group <= 8:
-            total = BR[level][0, rows, :].astype(F32)
-            for g in range(1, group):
-                total = total + BR[level][g, rows, :].astype(F32)
-            return total
-
-        def one(i, total):
-            for g in range(4):
-                total = total + BR[level][4 * i + g, rows, :].astype(F32)
-            return total
-
-        size = rows.size if hasattr(rows, "size") else rows.stop - rows.start
-        return lax.fori_loop(0, group // 4, one, jnp.zeros((size, B), F32))
+        group = BR[level].shape[0]
+        total = BR[level][0, rows, :].astype(F32)
+        for g in range(1, group):
+            total = total + BR[level][g, rows, :].astype(F32)
+        return total
 
     def await_chunks(level, copy):
         copy.wait()
-        await_bytes(BR[level].at[0 : GROUP[level] - 1], br.at[level])
+        await_bytes(BR[level].at[0 : BR[level].shape[0] - 1], br.at[level])
         size = CHUNK[level]
         return column_sum(gathered(level, slice(size, size + 16))) * (1.0 / D)
 
@@ -465,57 +445,53 @@
         if level == 0:
             share_grads(0)
             break
-        half, chunk = group // 2, CHUNK[level]
-        for side, dot in ((0, dl), (1, dr)):
-            tile = split_tile(column_sum(dot))
-            BS[level][side * half : (side + 1) * half, chunk : chunk + 16, :] = jnp.broadcast_to(
-                tile[None], (half, 16, B)
-            )
-
-        def part(t, carry):
-            rows = at(t, 256)
-            for side in range(2):
-                if level < 3:
-                    value = nn(WN[side, rows, col : col + w], GB[side, col : col + w, :])
-                else:
-                    value = nn(WN[side, rows, 896:1024], GP[level - 3, side])
-                value = value.astype(BF)
-                if chunk >= 256:
-                    per = chunk // 256
-                    BS[level][side * half + t // per, at(lax.rem(t, per), 256), :] = value
-                else:
-                    n = 256 // chunk
-                    BS[level][pl.ds(side * half + t * n, n), 0:chunk, :] = value.reshape(n, chunk, B)
-            return carry
-
-        lax.fori_loop(0, 4, part, 0)
+        chunk = CHUNK[level]
+        dots = [column_sum(dl), column_sum(dr)]
+
+        def half_sums(side, parity):
+            rows = pl.ds(pl.multiple_of(parity * 512, 512), 512)
+            if level == 1:
+                return nn(WN[side, rows, col : col + w], GB[side, col : col + w, :])
+            if level == 2:
+                return nn(WP[0, side, rows, :], GB[side, col : col + w, :])
+            return nn(WP[level - 2, side, rows, :], GP[level - 3, side])
+
+        for side in range(2):
+            BO[level - 1, side, 0:512, :] = half_sums(side, 1 - c).astype(BF)
+            BO[level - 1, side, 512:528, :] = split_tile(dots[side])
+        to_sub(BO.at[level - 1], BI.at[level - 1], bos.at[level], bis.at[level], partner)
+        for side in range(2):
+            PF[side] = half_sums(side, c)
+        await_bytes(BI.at[level - 1], bis.at[level])
+        quarter = group // 4
+        for side in range(2):
+            tile = split_tile(dots[side] + column_sum(BI[level - 1, side, 512:528, :].astype(F32)))
+            chunks = slice(side * quarter, (side + 1) * quarter)
+            value = (PF[side] + BI[level - 1, side, 0:512, :].astype(F32)).astype(BF)
+            BS[level][chunks, 0:chunk, :] = value.reshape(quarter, chunk, B)
+            BS[level][chunks, chunk : chunk + 16, :] = jnp.broadcast_to(tile[None], (quarter, 16, B))
         own_chunk = scatter(level, lax.rem(s, group))
         share_grads(level)
 
     await_bytes(MS.at[0:3], x2s)
 
-    def partial_sums(i):
-        src = source(i)
-        slot = i // 2 - i // 3
-        lanes = at(src, B)
-        if i:
-            await_bytes(GX.at[:, 0:512, lanes], gx0.at[src])
-
-        def other(t, carry):
-            rows = at(t, 256)
-            MS[src, rows, :] = nn(WN[1 - c, rows, 0:512], GX[1 - c, 0:512, lanes]).astype(BF)
-            return carry
-
-        def mine(t, carry):
-            rows = at(t, 256)
-            PM[slot, rows, :] = nn(WN[c, rows, 0:512], GX[c, 0:512, lanes])
-            return carry
-
-        lax.fori_loop(0, 4, other, 0)
-        to_sub(MS.at[src], PR.at[src], pss, prs.at[src], partner)
-        lax.fori_loop(0, 4, mine, 0)
-
-    partial_sums(0)
+    def partial_sums(blocks):
+        for i in blocks:
+            if i:
+                await_bytes(GX.at[:, 0:512, lanes_of(i)], gx0.at[i])
+        lanes = slice(blocks[0] * B, (blocks[-1] + 1) * B)
+        for t in range(4):
+            rows = slice(256 * t, 256 * (t + 1))
+            value = nn(WN[1 - c, rows, 0:512], GX[1 - c, 0:512, lanes]).astype(BF)
+            for b, i in enumerate(blocks):
+                MS[i, rows, :] = value[:, lanes_of(b)]
+        for i in blocks:
+            to_sub(MS.at[i], PR.at[i], pss, prs.at[i], partner)
+        for t in range(4):
+            rows = slice(256 * t, 256 * (t + 1))
+            PM[rows, 0 : B * len(blocks)] = nn(WN[c, rows, 0:512], GX[c, 0:512, lanes])
+
+    partial_sums((0,))
 
     for copy in kept:
         copy.wait()
@@ -527,13 +503,8 @@
     await_bytes(LO.at[:, 0 : 3 * B], x3r)
     await_bytes(H0.at[:, 0 : 3 * B], h0r)
 
-    def message_scale(t, total):
-        values = H0[at(t, 128), :].astype(F32)
-        return total + fold(values * values)
-
-    R0[...] = jnp.broadcast_to(
-        factor_of(lax.fori_loop(0, 8, message_scale, jnp.zeros((8, ALL), F32))), (8, ALL)
-    )
+    for i in range(REPS):
+        R0[:, lanes_of(i)] = jnp.broadcast_to(factor_of(squares_of(H0, 0, lanes_of(i))), (8, B))
 
     def await_grads(level):
         w, col = WIDTH[level], COLUMN[level]
@@ -555,55 +526,44 @@
         for side in range(2):
             OU[side, :, col : col + w] = nt(AX[level, side], GX[side, col : col + w, :]).astype(BF)
 
-    def leaf_back(i):
-        src = source(i)
-        slot = i // 2 - i // 3
-        lanes = at(src, B)
-        await_bytes(PR.at[src], prs.at[src])
-        scale0 = R0[0:1, lanes]
-
-        def add_parts(t, total):
-            rows = at(t, 128)
-            value = PM[slot, rows, :] + PR[src, rows, :].astype(F32)
-            PM[slot, rows, :] = value
-            return total + fold(value * H0[rows, lanes].astype(F32))
-
-        mean0 = column_sum(lax.fori_loop(0, 8, add_parts, jnp.zeros((8, B), F32))) * (1.0 / D)
-        shift = scale0 * scale0 * mean0
-
-        def mid_back(t, carry):
-            rows = at(t, 128)
-            v = PM[slot, rows, :] - H0[rows, lanes].astype(F32) * shift
-            CR[rows, lanes] = (v * LO[rows, lanes].astype(F32)).astype(BF)
-            return carry
-
-        lax.fori_loop(0, 8, mid_back, 0)
-
-        def product(t, total):
-            rows = at(t, 256)
+    def leaf_back(blocks):
+        lanes = slice(blocks[0] * B, (blocks[-1] + 1) * B)
+        n = B * len(blocks)
+        for i in blocks:
+            await_bytes(PR.at[i], prs.at[i])
+        for b, i in enumerate(blocks):
+            part = lanes_of(b)
+            total = jnp.zeros((8, B), F32)
+            for t in range(8):
+                rows = slice(128 * t, 128 * (t + 1))
+                value = PM[rows, part] + PR[i, rows, :].astype(F32)
+                PM[rows, part] = value
+                total = total + fold(value * H0[rows, lanes_of(i)].astype(F32))
+            scale0 = R0[0:1, lanes_of(i)]
+            shift = scale0 * scale0 * (column_sum(total) * (1.0 / D))
+            for t in range(8):
+                rows = slice(128 * t, 128 * (t + 1))
+                v = PM[rows, part] - H0[rows, lanes_of(i)].astype(F32) * shift
+                CR[rows, lanes_of(i)] = (v * LO[rows, lanes_of(i)].astype(F32)).astype(BF)
+        total = jnp.zeros((8, n), F32)
+        for t in range(4):
+            rows = slice(256 * t, 256 * (t + 1))
             value = nn(MW[rows, :], CR[:, lanes])
-            LB[rows, :] = value
-            return total + fold(value * LM[rows, lanes].astype(F32))
-
-        mean = column_sum(lax.fori_loop(0, 4, product, jnp.zeros((8, B), F32))) * (1.0 / D)
+            LB[rows, 0:n] = value
+            total = total + fold(value * LM[rows, lanes].astype(F32))
+        mean = column_sum(total) * (1.0 / D)
         r = RL[0:1, lanes]
-
-        def cotangents(t, carry):
-            rows = at(t, 128)
-            v = r * (LB[rows, :] - LM[rows, lanes].astype(F32) * mean)
-            rest = others([FK[k, rows, lanes] for k in range(4)])
+        for t in range(16):
+            rows = slice(64 * t, 64 * (t + 1))
+            v = r * (LB[rows, 0:n] - LM[rows, lanes].astype(F32) * mean)
+            rest = others([FK[k, rows, lanes].astype(F32) for k in range(4)])
             for k in range(4):
                 CT[k, rows, lanes] = (v * rest[k]).astype(BF)
-            return carry
-
-        lax.fori_loop(0, 8, cotangents, 0)
-
-    leaf_back(0)
-    partial_sums(1)
-    partial_sums(2)
-    leaf_back(1)
-    leaf_back(2)
-    partial_sums(3)
+
+    leaf_back((0,))
+    partial_sums((1, 2))
+    leaf_back((1, 2))
+    partial_sums((3,))
 
     rows = at(p, 256)
     OU[c, :, 0:512] = nt(H0[rows, :], GX[c, 0:512, :]).astype(BF)
@@ -618,7 +578,7 @@
     lax.fori_loop(0, 4, weave, 0)
     out_upper = pltpu.make_async_copy(OI, ug_hbm, out_sem.at[2])
     out_upper.start()
-    leaf_back(3)
+    leaf_back((3,))
 
     def leaf_gradient(k, carry):
         LW[k] = nt(XT[k], CT[k]).astype(BF)
@@ -641,6 +601,8 @@
     await_bytes(CS.at[0:3], x3s)
     await_bytes(H0.at[:, 0 : 3 * B], h0s)
     await_bytes(MS, pss)
+    for level in range(1, LEVELS):
+        await_bytes(BO.at[level - 1], bos.at[level])
     for level in range(LEVELS + 1):
         half = GROUP[level] // 2
         block = A[level].shape[0] // GROUP[level]
@@ -648,7 +610,7 @@
         if half > 1:
             await_bytes(A[level].at[0 : (half - 1) * block], ff.at[level])
         if level:
-            await_bytes(BS[level].at[0 : GROUP[level] - 1], bs.at[level])
+            await_bytes(BS[level].at[0 : BS[level].shape[0] - 1], bs.at[level])
         if 0 < level < LEVELS:
             await_bytes(AX.at[level, :, :, 0 : 3 * B], axs.at[level])
         else:
@@ -663,30 +625,33 @@
 def scratch():
     vm = pltpu.VMEM
     dma = pltpu.SemaphoreType.DMA
-    chunks = [vm((GROUP[j], CHUNK[j] + 16, B), BF) for j in range(1, LEVELS + 1)]
+    counts = [g // 2 for g in GROUP[:LEVELS]] + [SUBS]
+    chunks = [vm((counts[j], CHUNK[j] + 16, B), BF) for j in range(1, LEVELS + 1)]
     return (
         [
             vm((2048, F), BF), vm((256, 256), BF), vm((4, 4, B, F), BF), vm((4, ALL, F), BF),
             vm((4, F, D), BF), vm((4, D, F), BF), vm((D, D), BF), vm((D, D), BF),
             vm((D, 2, D), BF), vm((2, D, D), BF), vm((2, D, D), BF), vm((32, B), F32),
-            vm((4, D, ALL), F32), vm((8, ALL), F32), vm((D, ALL), BF),
+            vm((4, D, ALL), BF), vm((8, ALL), F32), vm((D, ALL), BF),
             vm((4, D, B), BF), vm((4, D, B), BF),
         ]
         + [vm((2 * D, B), BF)] * 5
         + [vm((D, B), BF)]
         + [vm((D, B), F32)] * 3
-        + [vm((3, 2, 128, B), BF), vm((2, D, B), BF)]
+        + [vm((3, 2, 128, B), BF), vm((2, D, B), BF), vm((3, 2, D, 128), BF)]
+        + [vm((4, 2, 528, B), BF)] * 2
+        + [vm((2, 512, B), F32)]
         + chunks
         + chunks
         + [
             vm((2, D, ALL), BF), vm((6, 2, 256, ALL), BF), vm((4, D, B), BF), vm((D, ALL), BF),
-            vm((D, B), F32), vm((4, D, ALL), BF), vm((4, F, ALL), BF), vm((2, 256, D), BF),
+            vm((D, 2 * B), F32), vm((4, D, ALL), BF), vm((4, F, ALL), BF), vm((2, 256, D), BF),
             vm((256, 2, D), BF), vm((D, ALL), BF), vm((D, ALL), BF), vm((8, ALL), F32),
-            vm((4, D, B), BF), vm((2, D, B), F32),
+            vm((4, D, B), BF), vm((D, 2 * B), F32),
         ]
         + [
             dma((5,)), dma((22,)), dma, dma((4,)), dma, dma, dma, dma, dma, dma,
-            dma((6,)), dma((6, 16)), dma((6,)), dma((6,)), dma((6,)), dma((6,)),
+            dma((6,)), dma((6, 16)), dma((6,)), dma((6,)), dma((6,)), dma((6,)), dma((6,)), dma((6,)),
             dma((6,)), dma((6,)), dma((6,)), dma((6,)), dma((4,)), dma, dma((4,)), dma((3,)),
         ]
     )

time: 159 us -> 144 us (0.906)
  Pallas kernels: 152 us -> 137 us
    pallas_call x1, Pallas kernels: 152 us -> 137 us  [on_device(): pl.pallas_call(kernel, out_shape=(jax.ShapeDtypeStruct((4, F, D), BF), ja...]
where the time goes in v3:
time: 144 us
  Pallas kernels  137 us (95%)
  local copies, waits for them, and re-layouts  6.16 us (4%)
    pallas_call x1, Pallas kernels, on_device(): pl.pallas_call(kernel, out_shape=(jax.ShapeDtypeStruct((4, F, D), BF), ja...  137 us
    unnamed x7, local copies, waits for them, and re-layouts  6.16 us

profile of v3, /device:TPU:1, one launch (start us, length us, event | category | flops | bytes accessed | tf_op | source)
XLA Modules:
  0.0 143.7 jit_solution(6840619289532902424)
XLA Ops:
  0.6 136.9 %shard_map.85 = (bf16[4,256,1024]{2,1,0:T(8,128)(2,1)}, bf16[1024,1024]{1,0:T(8,128)(2,1)}, bf16[256,2,1024]{2,1,0:T(2,128)(2,1)}) custom-call(s32[16]{0:T(128)} %map_ref.1, bf16[2048,256]{1,0:T(8,128)(2,1)} %bitcast.13, bf16[4,256,1024]{2,1,0:T(8,128)(2,1)} %bitcast.9, bf16[1024,1024]{1,0:T(8,128)(2,1)} %bitcast.10, bf16[1024,2,1024]{2,1,0:T(2,128)(2,1)} %bitcast.8, ...), custom_call_target="tpu_custom_call" | custom-call | tf_op jit(solution)/shard_map/pallas_call | solution.py:662
  137.5 0.0 copy-start
  137.6 3.2 %copy.12 = bf16[1,4,256,1024]{3,2,1,0:T(8,128)(2,1)} copy(bf16[1,4,256,1024]{3,2,1,0:T(8,128)(2,1)} %bitcast.12) | data formatting | bytes 4194304
  140.8 0.0 copy-done
  140.8 0.0 copy-start.1
  140.8 1.3 copy.13
  142.1 0.6 copy-done.1
  142.7 1.0 copy.14
Async XLA Ops:
  137.5 3.2 %copy-start = (bf16[1024,1024]{1,0:T(8,128)(2,1)S(1)}, bf16[1024,1024]{1,0:T(8,128)(2,1)}, u32[]{:S(2)}) copy-start(bf16[1024,1024]{1,0:T(8,128)(2,1)} %get-tuple-element.7) | copy-start | bytes 6291460
  140.8 2.0 %copy-start.1 = (bf16[256,2,1024]{2,1,0:T(2,128)(2,1)S(1)}, bf16[256,2,1024]{2,1,0:T(2,128)(2,1)}, u32[]{:S(2)}) copy-start(bf16[256,2,1024]{2,1,0:T(2,128)(2,1)} %get-tuple-element.8) | copy-start | bytes 3145732
